TPU v7x, 256 devices: a whole 4x4x8 slice. The times are simulated.
256 devices in a mesh: gx: 32 (over y_hi, z, core), gy: 8 (over y_lo, x).
Axes of the slice: x: 4, y: 4 (y_hi: 2, y_lo: 2; y = y_hi * 2 + y_lo), z: 8, core: 2. Of those that a mesh axis runs over, the one named last changes fastest.
Arguments:
- state_field: bfloat16 [1, 64, 2048, 2048], P(None, None, 'gx', 'gy'), may hold values from -6 to 6
- spectral_x: bfloat16 [2, 32, 2, 64, 64], P(None, 'gx'), may hold values from -2 to 2
- spectral_y: bfloat16 [2, 32, 2, 64, 64], P(None, 'gy'), may hold values from -2 to 2
- expand_weight: bfloat16 [2, 64, 256], replicated, may hold values from -0.75 to 0.75
- reduce_weight: bfloat16 [2, 256, 64], replicated, may hold values from -0.375 to 0.375
Outputs:
- next_state: bfloat16 [1, 64, 2048, 2048], P(None, None, 'gx', 'gy')
All inputs are finite; a program needn't handle non-finite values.
Results may differ from a plain program's by a relative error of at most 0.025.
Values may be sent and summed in bfloat16 or wider, within the bound.
No kernel may reach another device: no remote copies, remote signals or barrier semaphores. Data moves between devices by JAX's collectives and lax.ppermute only.
A program may use at most 64 MiB of HBM per device.

v0:
```python
import jax
import jax.numpy as jnp
from jax import lax
from jax.sharding import PartitionSpec as P

NX = 2048
NY = 2048
MODES = 32
LAYERS = 2


def make_tables(length, modes):
    positions = jnp.arange(length, dtype=jnp.int32)
    orders = jnp.arange(modes, dtype=jnp.int32)
    phase = orders[:, None] * positions[None, :] % length
    angle = 2.0 * jnp.pi * phase.astype(jnp.float32) / length
    factor = 1.0 / jnp.sqrt(jnp.float32(length))
    weight_two = jnp.where(orders == 0, 1.0, 2.0).astype(jnp.float32)[:, None]
    forward = jnp.stack([jnp.cos(angle) * factor, -jnp.sin(angle) * factor], axis=1)
    forward = forward.reshape(2 * modes, length).astype(jnp.bfloat16)
    inverse = jnp.stack(
        [weight_two * jnp.cos(angle) * factor, -weight_two * jnp.sin(angle) * factor], axis=1
    )
    inverse = inverse.reshape(2 * modes, length).T.astype(jnp.bfloat16)
    return (forward, inverse)


def mix_modes(spectrum, weights):
    modes = weights.shape[0]
    shaped = spectrum.reshape((modes, 2) + spectrum.shape[1:])
    real_in, imag_in = (shaped[:, 0], shaped[:, 1])
    real_w, imag_w = (weights[:, 0], weights[:, 1])

    def contract_modes(left, right):
        return jnp.einsum("koi,kzin->kzon", left, right, preferred_element_type=jnp.float32)

    real_out = contract_modes(real_w, real_in) - contract_modes(imag_w, imag_in)
    imag_out = contract_modes(real_w, imag_in) + contract_modes(imag_w, real_in)
    joined = jnp.stack([real_out, imag_out], axis=1).astype(jnp.bfloat16)
    return joined.reshape(spectrum.shape)


def body(state_field, spectral_x, spectral_y, expand_weight, reduce_weight):
    planes, channels, local_rows, local_cols = state_field.shape
    row_first = lax.axis_index("gx") * local_rows
    col_first = lax.axis_index("gy") * local_cols
    forward_x, inverse_x = make_tables(NX, MODES)
    forward_y, inverse_y = make_tables(NY, MODES)
    forward_xloc = lax.dynamic_slice_in_dim(forward_x, row_first, local_rows, 1)
    inverse_xloc = lax.dynamic_slice_in_dim(inverse_x, row_first, local_rows, 0)
    forward_yloc = lax.dynamic_slice_in_dim(forward_y, col_first, local_cols, 1)
    inverse_yloc = lax.dynamic_slice_in_dim(inverse_y, col_first, local_cols, 0)
    state = state_field
    for layer_index in range(LAYERS):
        weights_x = spectral_x[layer_index]
        weights_y = spectral_y[layer_index]
        spec_x = lax.psum_scatter(
            jnp.einsum(
                "kx,zcxy->kzcy", forward_xloc, state, preferred_element_type=jnp.float32
            ).astype(jnp.bfloat16),
            "gx",
            scatter_dimension=0,
            tiled=True,
        )
        spec_y = lax.psum_scatter(
            jnp.einsum(
                "ky,zcxy->kzcx", forward_yloc, state, preferred_element_type=jnp.float32
            ).astype(jnp.bfloat16),
            "gy",
            scatter_dimension=0,
            tiled=True,
        )
        mixed_x = mix_modes(spec_x, weights_x)
        mixed_y = mix_modes(spec_y, weights_y)
        branch_x = jnp.einsum(
            "xk,kzcy->zcxy",
            inverse_xloc,
            lax.all_gather(mixed_x, "gx", axis=0, tiled=True),
            preferred_element_type=jnp.float32,
        ).astype(jnp.bfloat16)
        branch_y = jnp.einsum(
            "yk,kzcx->zcxy",
            inverse_yloc,
            lax.all_gather(mixed_y, "gy", axis=0, tiled=True),
            preferred_element_type=jnp.float32,
        ).astype(jnp.bfloat16)
        total = (branch_x.astype(jnp.float32) + branch_y.astype(jnp.float32)).astype(jnp.bfloat16)
        hidden = jax.nn.gelu(
            jnp.einsum(
                "ch,zcxy->zhxy",
                expand_weight[layer_index],
                total,
                preferred_element_type=jnp.float32,
            ),
            approximate=True,
        )
        hidden = hidden.astype(jnp.bfloat16)
        update = jnp.einsum(
            "hc,zhxy->zcxy", reduce_weight[layer_index], hidden, preferred_element_type=jnp.float32
        )
        state = (state.astype(jnp.float32) + update).astype(jnp.bfloat16)
    return state


def solution(mesh):
    in_specs = (
        P(None, None, "gx", "gy"),
        P(None, "gx", None, None, None),
        P(None, "gy", None, None, None),
        P(),
        P(),
    )
    out_specs = P(None, None, "gx", "gy")
    return jax.shard_map(body, mesh=mesh, in_specs=in_specs, out_specs=out_specs, check_vma=False)
```

profile of v0, /device:TPU:1, one launch (start us, length us, event | category | flops | bytes accessed | tf_op | source)
XLA Modules:
  0.0 543.5 jit_solution(1677750337479074670)
XLA Ops:
  6.5 1.1 multiply_convert_fusion.2
  7.7 0.3 copy.123
  7.9 0.1 convert_element_type.184
  8.1 2.3 convert_bitcast_fusion.3
  10.4 2.5 copy.124
  12.9 0.0 reduce-scatter.9.cloned.1.call-update
  12.9 0.0 reduce-scatter.13.cloned.1.call-start
  13.0 1.5 copy-done
  14.5 1.1 fusion.63
  15.6 0.7 copy.153
  16.3 1.6 reshape.480
  18.0 0.0 all-gather.3.cloned.1.call-start
  18.0 0.6 slice_bitcast_fusion.28
  18.6 112.1 %reduce-scatter.9.cloned.1.call-done = bf16[2,1,64,256]{3,2,1,0:T(8,128)(2,1)} async-done(((bf16[64,1,64,256]{3,2,1,0:T(8,128)(2,1)}), bf16[2,1,64,256]{3,2,1,0:T(8,128)(2,1)}) %reduce-scatter.9.cloned.1.call-update) | async-done | bytes 65552 | tf_op jit(solution)/shard_map/reduce_scatter | solution.py:57
  130.7 0.9 fusion.118
  131.6 0.9 fusion.83
  132.5 0.9 fusion.117
  133.4 0.9 fusion.84
  134.3 0.6 pad_maximum_fusion.4
  134.9 0.0 reduce-scatter.11.cloned.1.call-start
  135.1 1.0 multiply_convert_fusion
  136.1 1.0 multiply_convert_fusion.1
  137.1 0.3 copy.126
  137.4 0.8 convert_element_type.187
  138.2 33.9 %reduce-scatter.13.cloned.1.call-done = bf16[8,4096]{1,0:T(8,128)(2,1)} async-done(((bf16[64,4096]{1,0:T(8,128)(2,1)}), bf16[8,4096]{1,0:T(8,128)(2,1)}) %reduce-scatter.13.cloned.1.call-update) | async-done | bytes 65552
  172.1 1.0 reshape.481
  173.1 0.2 fusion.97
  173.3 0.2 fusion.76
  173.5 0.2 fusion.98
  173.7 0.2 fusion.75
  174.0 0.1 copy.132
  174.1 24.2 %all_gather.13 = bf16[64,1,64,64]{3,2,1,0:T(8,128)(2,1)S(1)} all-gather(bf16[8,1,64,64]{3,2,1,0:T(8,128)(2,1)S(1)} %bitcast.306), channel_id=1, replica_groups=mesh['gx'=32,'gy'=8] {'gy'}, dimensions={0}, use_global_device_ids=true | all-gather | bytes 589824 | tf_op jit(solution)/shard_map/all_gather | solution.py:84
  198.3 1.2 copy.134
  199.5 1.4 fusion.87
  201.0 58.1 %all-gather.3.cloned.1.call-done = bf16[64,1,64,256]{3,2,1,0:T(8,128)(2,1)} async-done(((bf16[2,1,64,256]{3,2,1,0:T(8,128)(2,1)}), bf16[64,1,64,256]{3,2,1,0:T(8,128)(2,1)}) %all-gather.3.cloned.1.call-update) | async-done | bytes 2097168 | tf_op jit(solution)/shard_map/all_gather | solution.py:78
  259.1 4.7 fusion.24
  263.9 12.2 %fusion.22 = bf16[1,64,64,256]{3,1,2,0:T(8,128)(2,1)S(1)} fusion(bf16[1,64,64,256]{3,2,1,0:T(8,128)(2,1)} %param.5, bf16[64,64,256]{2,1,0:T(8,128)(2,1)} %fusion.24, bf16[2,256,64]{1,2,0:T(8,128)(2,1)S(1)} %copy-done.5, bf16[2,64,256]{2,1,0:T(8,128)(2,1)S(1)} %copy-done.7), kind=kOutput, calls=%fused_computation.28 | convolution fusion | flops 1114636288 | bytes 6356992 | tf_op jit(solution)/shard_map/hc,zhxy->zcxy/dot_general | solution.py:98
  276.1 1.7 convert_bitcast_fusion.2
  277.9 2.5 copy.138
  280.4 0.3 reduce-scatter.15.cloned.1.call-start
  280.7 2.6 fusion.66
  283.3 0.7 copy.155
  284.0 1.6 reshape.482
  285.6 0.0 all-gather.5.cloned.1.call-start
  285.7 105.2 %reduce-scatter.11.cloned.1.call-done = bf16[2,1,64,256]{3,2,1,0:T(8,128)(2,1)} async-done(((bf16[64,1,64,256]{3,2,1,0:T(8,128)(2,1)}), bf16[2,1,64,256]{3,2,1,0:T(8,128)(2,1)}) %reduce-scatter.11.cloned.1.call-update) | async-done | bytes 65552 | tf_op jit(solution)/shard_map/reduce_scatter | solution.py:57
  390.9 0.9 fusion.119
  391.7 0.9 fusion.82
  392.6 0.9 fusion.120
  393.5 0.9 fusion.81
  394.4 0.6 pad_maximum_fusion.5
  395.1 36.6 %reduce-scatter.15.cloned.1.call-done = bf16[8,4096]{1,0:T(8,128)(2,1)} async-done(((bf16[64,4096]{1,0:T(8,128)(2,1)}), bf16[8,4096]{1,0:T(8,128)(2,1)}) %reduce-scatter.15.cloned.1.call-update) | async-done | bytes 65552
  431.7 1.0 reshape.483
  432.7 0.2 fusion.99
  433.0 0.2 fusion.74
  433.2 0.2 fusion.100
  433.4 0.2 fusion.73
  433.6 0.1 copy.145
  433.8 24.0 %all_gather.15 = bf16[64,1,64,64]{3,2,1,0:T(8,128)(2,1)S(1)} all-gather(bf16[8,1,64,64]{3,2,1,0:T(8,128)(2,1)S(1)} %bitcast.307), channel_id=1, replica_groups=mesh['gx'=32,'gy'=8] {'gy'}, dimensions={0}, use_global_device_ids=true | all-gather | bytes 589824 | tf_op jit(solution)/shard_map/all_gather | solution.py:84
  457.8 1.2 copy.147
  459.0 1.4 fusion.85
  460.5 58.2 %all-gather.5.cloned.1.call-done = bf16[64,1,64,256]{3,2,1,0:T(8,128)(2,1)} async-done(((bf16[2,1,64,256]{3,2,1,0:T(8,128)(2,1)}), bf16[64,1,64,256]{3,2,1,0:T(8,128)(2,1)}) %all-gather.5.cloned.1.call-update) | async-done | bytes 2097168 | tf_op jit(solution)/shard_map/all_gather | solution.py:78
  518.7 4.7 fusion.25
  523.4 10.8 %fusion.20 = bf16[1,64,64,256]{3,1,2,0:T(8,128)(2,1)S(1)} fusion(bf16[1,64,64,256]{3,1,2,0:T(8,128)(2,1)} %copy-done.1, bf16[64,64,256]{2,1,0:T(8,128)(2,1)} %fusion.25, bf16[2,256,64]{1,2,0:T(8,128)(2,1)S(1)} %copy-done.6, bf16[2,64,256]{2,1,0:T(8,128)(2,1)S(1)} %copy-done.8), kind=kOutput, calls=%fused_computation.23 | convolution fusion | flops 1114636288 | bytes 6356992 | tf_op jit(solution)/shard_map/hc,zhxy->zcxy/dot_general | solution.py:98
  534.2 2.5 copy.150
  (31 shorter events, 0.3 us)
Async XLA Ops:
  6.5 124.2 %reduce-scatter.9.cloned.1.call-start = ((), (), s32[]{:S(2)}) async-start(), calls=%async_computation.4 | async-start | bytes 2162688 | tf_op jit(solution)/shard_map/reduce_scatter | solution.py:57
  12.9 1.6 copy-start
  12.9 159.1 %reduce-scatter.13.cloned.1.call-start = ((), (), s32[]{:S(2)}) async-start(), calls=%async_computation.8 | async-start | bytes 589824
  15.6 2.4 copy-start.4
  15.6 119.4 %copy-start.3 = (bf16[2,4,2,64,64]{4,3,2,1,0:T(8,128)(2,1)S(1)}, bf16[2,4,2,64,64]{4,3,2,1,0:T(8,128)(2,1)}, u32[]{:S(2)}) copy-start(bf16[2,4,2,64,64]{4,3,2,1,0:T(8,128)(2,1)} %param.7) | copy-start | bytes 393220
  18.0 241.2 %all-gather.3.cloned.1.call-start = ((), (), s32[]{:S(2)}) async-start(), calls=%async_computation.5 | async-start | bytes 2162688 | tf_op jit(solution)/shard_map/all_gather | solution.py:78
  134.9 255.9 %reduce-scatter.11.cloned.1.call-start = ((), (), s32[]{:S(2)}) async-start(), calls=%async_computation.6 | async-start | bytes 2162688 | tf_op jit(solution)/shard_map/reduce_scatter | solution.py:57
  201.0 62.9 %copy-start.5 = (bf16[2,256,64]{1,2,0:T(8,128)(2,1)S(1)}, bf16[2,256,64]{1,2,0:T(8,128)(2,1)}, u32[]{:S(2)}) copy-start(bf16[2,256,64]{1,2,0:T(8,128)(2,1)} %param.9) | copy-start | bytes 196612
  201.0 62.9 %copy-start.7 = (bf16[2,64,256]{2,1,0:T(8,128)(2,1)S(1)}, bf16[2,64,256]{2,1,0:T(8,128)(2,1)}, u32[]{:S(2)}) copy-start(bf16[2,64,256]{2,1,0:T(8,128)(2,1)} %param.8) | copy-start | bytes 196612
  276.1 4.6 copy-start.1
  280.4 151.3 %reduce-scatter.15.cloned.1.call-start = ((), (), s32[]{:S(2)}) async-start(), calls=%async_computation.9 | async-start | bytes 589824
  283.3 107.5 %copy-start.2 = (bf16[1,2,64,64]{3,2,1,0:T(8,128)(2,1)S(1)}, bf16[1,2,64,64]{3,2,1,0:T(8,128)(2,1)}, u32[]{:S(2)}) copy-start(bf16[1,2,64,64]{3,2,1,0:T(8,128)(2,1)} %get-tuple-element.7) | copy-start | bytes 49156
  285.6 233.0 %all-gather.5.cloned.1.call-start = ((), (), s32[]{:S(2)}) async-start(), calls=%async_computation.7 | async-start | bytes 2162688 | tf_op jit(solution)/shard_map/all_gather | solution.py:78
  460.5 62.9 %copy-start.6 = (bf16[2,256,64]{1,2,0:T(8,128)(2,1)S(1)}, bf16[2,256,64]{1,2,0:T(8,128)(2,1)}, u32[]{:S(2)}) copy-start(bf16[2,256,64]{1,2,0:T(8,128)(2,1)} %param.9) | copy-start | bytes 196612
  460.5 62.9 %copy-start.8 = (bf16[2,64,256]{2,1,0:T(8,128)(2,1)S(1)}, bf16[2,64,256]{2,1,0:T(8,128)(2,1)}, u32[]{:S(2)}) copy-start(bf16[2,64,256]{2,1,0:T(8,128)(2,1)} %param.8) | copy-start | bytes 196612
Sparse Core Ops, SparseCore 0:
  13.1 117.6 reduce-scatter.8
  133.4 38.6 reduce-scatter.12
  174.8 84.2 all-gather.2
  280.5 110.2 reduce-scatter.10
  393.4 38.2 reduce-scatter.14
  434.3 84.2 all-gather.4
where the time goes:
time: 545 us; the launch traced here: 544 us
  waiting for transfers between devices  404 us (74%)
  matrix products  51.9 us (10%)
  blocking collectives  48.2 us (9%)
  local copies, waits for them, and re-layouts  20.5 us (4%)
  between operations  13.8 us (3%)
    reduce_scatter x2, waiting for transfers between devices, body(): lax.psum_scatter(jnp.einsum('kx,zcxy->kzcy', forward_xloc, state, preferr...  217 us
    all_gather x2, waiting for transfers between devices, body(): lax.all_gather(mixed_x, 'gx', axis=0, tiled=True)  116 us
    unnamed x8, waiting for transfers between devices  70.6 us
    all_gather x2, blocking collectives, body(): lax.all_gather(mixed_y, 'gy', axis=0, tiled=True)  48.2 us
    dot_general x2, matrix products, body(): jnp.einsum('hc,zhxy->zcxy', reduce_weight[layer_index], hidden, preferred...  23 us
  transfers between devices with their start and end apart: 6, of which 6 were waited for; matrix products, arithmetic and copies ran while one was open for 5% of the time, Pallas kernels for 0%

commit v1 on v0

v1 whole, which is shorter than its diff:
```python
import functools

import jax
import jax.numpy as jnp
import numpy as np
from jax import lax
from jax.experimental import pallas as pl
from jax.experimental.pallas import tpu as pltpu
from jax.sharding import PartitionSpec as P

F32 = jnp.float32
BF16 = jnp.bfloat16
NX = 2048
NY = 2048
CH = 64
HID = 256
MODES = 32
LAYERS = 2
RX = 10
RY = 20
RYP = 24
LINE = 8


def window_tables(length, devices, rank):
    window = length // devices
    k = np.arange(MODES)[:, None]
    p = np.arange(length)[None, :]
    angle = 2.0 * np.pi * ((k * p) % length) / length
    scale = 1.0 / np.sqrt(length)
    weight = np.where(np.arange(MODES) == 0, 1.0, 2.0)[:, None]
    forward = np.concatenate([np.cos(angle), -np.sin(angle)], 0) * scale
    inverse = np.concatenate([weight * np.cos(angle), -weight * np.sin(angle)], 0) * scale
    _, _, vt = np.linalg.svd(forward[:, :window], full_matrices=False)
    basis = vt[:rank]
    basis = basis * np.sign(basis[np.arange(rank), np.abs(basis).argmax(1)])[:, None]
    fwd = np.stack([forward[:, d * window : (d + 1) * window] @ basis.T for d in range(devices)])
    inv = np.stack([inverse[:, d * window : (d + 1) * window] @ basis.T for d in range(devices)])
    return basis, fwd, inv


def bf(x):
    return np.asarray(x, np.float32).astype(jnp.bfloat16)


def make_constants():
    bx, fx, ix = window_tables(NX, 32, RX)
    by, fy, iy = window_tables(NY, 8, RY)
    pairs = RX // 2
    ax = fx.reshape(32, 64, pairs, 2).transpose(3, 1, 2, 0).reshape(128, pairs * 32)
    gx = ix.reshape(32, 2, MODES, pairs, 2)
    u0 = gx[..., 0].transpose(3, 0, 1, 2).reshape(pairs * 32, 64)
    u1 = gx[..., 1].transpose(3, 0, 1, 2)[:, :, ::-1].reshape(pairs * 32, 64)
    ux = np.concatenate([u0, u1], 0)
    pad = ((0, 0), (0, 0), (0, RYP - RY))
    fy, iy = np.pad(fy, pad), np.pad(iy, pad)
    ay = fy.transpose(1, 0, 2).reshape(64, 8 * RYP)
    gy = iy.transpose(0, 2, 1).reshape(8 * RYP, 64)
    cy = np.pad(by, ((0, RYP - RY), (0, 0)))
    bexp = np.repeat(bx, CH, axis=1)
    bexp = np.pad(bexp, ((0, 16 - RX), (0, 0)))
    return dict(
        ax=bf(ax), ux=bf(ux), ay=bf(ay), gy=bf(gy), cy=bf(cy), cyt=bf(cy.T), bexp=bf(bexp)
    )


def dot(a, b):
    return jnp.dot(a, b, preferred_element_type=F32)


def dot_nt(a, b):
    return lax.dot_general(a, b, (((1,), (1,)), ((), ())), preferred_element_type=F32)


def half_mask(rows):
    return lax.broadcasted_iota(jnp.int32, (rows, 128), 1) < 64


def first_kernel(state_ref, bexp_ref, cy_ref, kron_ref, zx_ref, zy_ref, acc_ref):
    g = pl.program_id(0)
    lanes = lax.broadcasted_iota(jnp.int32, (CH, 512), 1)
    rows = lax.broadcasted_iota(jnp.int32, (CH, 512), 0)
    eye = (lanes % CH) == rows
    for r in range(RX):
        row = jnp.broadcast_to(bexp_ref[r : r + 1, :].astype(F32), (CH, 512))
        kron_ref[r * CH : (r + 1) * CH, :] = jnp.where(eye, row, 0.0).astype(BF16)
    state = state_ref[...]
    part = dot_nt(state, kron_ref[...])

    @pl.when(g == 0)
    def _():
        acc_ref[...] = part

    @pl.when(g > 0)
    def _():
        acc_ref[...] += part

    zy_ref[0] = dot(cy_ref[...], state).astype(BF16)

    @pl.when(g == pl.num_programs(0) - 1)
    def _():
        zx_ref[...] = acc_ref[...].astype(BF16)


def first_call(state, c):
    return pl.pallas_call(
        first_kernel,
        name="first",
        grid=(8,),
        in_specs=[
            pl.BlockSpec((256, 512), lambda g: (0, g)),
            pl.BlockSpec((16, 512), lambda g: (0, g)),
            pl.BlockSpec((RYP, 256), lambda g: (0, 0)),
        ],
        out_specs=[
            pl.BlockSpec((RX * CH, 512), lambda g: (0, g)),
            pl.BlockSpec((256, RX * CH), lambda g: (0, 0)),
            pl.BlockSpec((1, RYP, 512), lambda g: (g, 0, 0)),
        ],
        out_shape=[
            jax.ShapeDtypeStruct((RX * CH, 4096), BF16),
            jax.ShapeDtypeStruct((256, RX * CH), BF16),
            jax.ShapeDtypeStruct((8, RYP, 512), BF16),
        ],
        scratch_shapes=[pltpu.VMEM((256, RX * CH), F32)],
        compiler_params=pltpu.CompilerParams(vmem_limit_bytes=48 << 20),
    )(state, c["bexp"], c["cy"])


def mix(xs_ref, ms_ref, core_ref, weight_refs):
    sign = jnp.where(half_mask(CH), 1.0, -1.0)
    for other, w_ref in enumerate(weight_refs):
        core = core_ref[0] if other == 0 else 1 - core_ref[0]
        groups, _, run = w_ref.shape[:3]
        for group in range(groups):
            for place in range(run):
                w = w_ref[group, 0, place].astype(F32)
                full = jnp.concatenate([w * sign, pltpu.roll(w, 64, 1)], axis=0).astype(BF16)
                mode = (group * 2 + core) * run + place
                rows = pl.ds(pl.multiple_of(mode * LINE, LINE), LINE)
                ms_ref[rows, :] = dot_nt(xs_ref[rows, :].astype(BF16), full)


def mid_x_kernel(
    core_ref, recv_ref, w0_ref, w1_ref, ax_ref, ux_ref, send_ref, r_ref, xs_ref, ms_ref, o_ref
):
    pairs = RX // 2
    first = half_mask(MODES)
    for p in range(pairs):
        part = recv_ref[:, :, p * 128 : (p + 1) * 128]
        r_ref[p] = part.reshape(256, 128).astype(F32)
    cols = []
    for y in range(LINE):
        ry = [r_ref[p, pl.ds(y, 32, stride=LINE), :] for p in range(pairs)]
        cols.append(jnp.concatenate(ry, axis=0).astype(BF16))
    spec = dot(ax_ref[...], jnp.concatenate(cols, axis=1))
    for y in range(LINE):
        s = spec[:, y * 128 : (y + 1) * 128]
        x = jnp.where(first, s[0:32], s[96:128])
        x = x + pltpu.roll(jnp.where(first, s[32:64], s[64:96]), 64, 1)
        xs_ref[pl.ds(y, MODES, stride=LINE), :] = x
    mix(xs_ref, ms_ref, core_ref, (w0_ref, w1_ref))
    cols = []
    for y in range(LINE):
        m = ms_ref[pl.ds(y, MODES, stride=LINE), :]
        cols.append(jnp.concatenate([m, pltpu.roll(m, 64, 1)], axis=0).astype(BF16))
    out = dot(ux_ref[...], jnp.concatenate(cols, axis=1))
    for y in range(LINE):
        for p in range(pairs):
            v0 = out[p * 32 : (p + 1) * 32, y * 128 : (y + 1) * 128]
            v1 = out[(pairs + p) * 32 : (pairs + p + 1) * 32, y * 128 : (y + 1) * 128]
            o_ref[p, pl.ds(y, 32, stride=LINE), :] = jnp.where(first, v0, v1)
    for p in range(pairs):
        part = o_ref[p].reshape(32, LINE, 128).astype(BF16)
        send_ref[:, :, p * 128 : (p + 1) * 128] = part


def mid_specs(recv, w, tables, layer):
    whole = lambda a: pl.BlockSpec(a.shape, lambda *_: (0,) * a.ndim)
    weights = pl.BlockSpec((w.shape[0], 1) + w.shape[2:], lambda *_: (0, layer, 0, 0, 0))
    return (
        [pl.BlockSpec(memory_space=pltpu.SMEM), whole(recv), weights, weights]
        + [whole(t) for t in tables],
        whole(recv),
    )


def mid_x(core, recv, w, c, layer):
    in_specs, out_specs = mid_specs(recv, w[0], (c["ax"], c["ux"]), layer)
    return pl.pallas_call(
        mid_x_kernel,
        name="mid_x",
        grid=(1,),
        in_specs=in_specs,
        out_specs=out_specs,
        out_shape=jax.ShapeDtypeStruct(recv.shape, BF16),
        scratch_shapes=[
            pltpu.VMEM((RX // 2, 256, 128), F32),
            pltpu.VMEM((MODES * LINE, 128), F32),
            pltpu.VMEM((MODES * LINE, 128), F32),
            pltpu.VMEM((RX // 2, 256, 128), F32),
        ],
        compiler_params=pltpu.CompilerParams(vmem_limit_bytes=48 << 20),
    )(core, recv, w[0], w[1], c["ax"], c["ux"])


def mid_y_kernel(core_ref, recv_ref, w0_ref, w1_ref, ay_ref, gy_ref, send_ref, xs_ref, ms_ref):
    first = half_mask(MODES)
    spec = dot(ay_ref[...], recv_ref[...].reshape(8 * RYP, 512))
    for b in range(LINE // 2):
        re = spec[0:32, b * 128 : (b + 1) * 128]
        im = spec[32:64, b * 128 : (b + 1) * 128]
        xs_ref[pl.ds(2 * b, MODES, stride=LINE), :] = jnp.where(first, re, pltpu.roll(im, 64, 1))
        xs_ref[pl.ds(2 * b + 1, MODES, stride=LINE), :] = jnp.where(
            first, pltpu.roll(re, 64, 1), im
        )
    mix(xs_ref, ms_ref, core_ref, (w0_ref, w1_ref))
    cols = []
    for b in range(LINE // 2):
        m0 = ms_ref[pl.ds(2 * b, MODES, stride=LINE), :]
        m1 = ms_ref[pl.ds(2 * b + 1, MODES, stride=LINE), :]
        re = jnp.where(first, m0, pltpu.roll(m1, 64, 1))
        im = jnp.where(first, pltpu.roll(m0, 64, 1), m1)
        cols.append(jnp.concatenate([re, im], axis=0).astype(BF16))
    out = dot(gy_ref[...], jnp.concatenate(cols, axis=1))
    send_ref[...] = out.reshape(8, RYP, 512).astype(BF16)


def mid_y(core, recv, w, c, layer):
    in_specs, out_specs = mid_specs(recv, w[0], (c["ay"], c["gy"]), layer)
    return pl.pallas_call(
        mid_y_kernel,
        name="mid_y",
        grid=(1,),
        in_specs=in_specs,
        out_specs=out_specs,
        out_shape=jax.ShapeDtypeStruct(recv.shape, BF16),
        scratch_shapes=[
            pltpu.VMEM((MODES * LINE, 128), F32),
            pltpu.VMEM((MODES * LINE, 128), F32),
        ],
        compiler_params=pltpu.CompilerParams(vmem_limit_bytes=48 << 20),
    )(core, recv, w[0], w[1], c["ay"], c["gy"])


def gelu(x):
    inner = x * (0.7978845608028654 + 0.035677408136300125 * (x * x))
    half = 0.5 * x
    return half + half * jnp.tanh(inner)


def last_kernel(more, *refs):
    yx_ref, kron_ref, yy_ref, cyt_ref, state_ref, we_ref, wr_ref = refs[:7]
    if more:
        cy_ref, out_ref, zx_ref, zy_ref, we4_ref, wr4_ref, acc_ref = refs[7:]
    else:
        out_ref, we4_ref, wr4_ref = refs[7:]
    g = pl.program_id(0)

    @pl.when(g == 0)
    def _():
        we4_ref[...] = jnp.zeros_like(we4_ref)
        wr4_ref[...] = jnp.zeros_like(wr4_ref)
        for j in range(4):
            we4_ref[j * CH : (j + 1) * CH, j * HID : (j + 1) * HID] = we_ref[...]
            wr4_ref[j * HID : (j + 1) * HID, j * CH : (j + 1) * CH] = wr_ref[...]

    kron = kron_ref[...]
    total = dot(yx_ref[...], kron) + dot(cyt_ref[...], yy_ref[0])
    total = total.astype(BF16)
    for j in range(2):
        part = total[:, j * 256 : (j + 1) * 256]
        hidden = gelu(dot(part, we4_ref[...])).astype(BF16)
        update = dot(hidden, wr4_ref[...])
        old = state_ref[:, j * 256 : (j + 1) * 256].astype(F32)
        out_ref[:, j * 256 : (j + 1) * 256] = (old + update).astype(BF16)
    if more:
        state = out_ref[...]
        part = dot_nt(state, kron)

        @pl.when(g == 0)
        def _():
            acc_ref[...] = part

        @pl.when(g > 0)
        def _():
            acc_ref[...] += part

        zy_ref[0] = dot(cy_ref[...], state).astype(BF16)

        @pl.when(g == pl.num_programs(0) - 1)
        def _():
            zx_ref[...] = acc_ref[...].astype(BF16)


def last_call(more, yx, kron, yy, state, we, wr, c):
    in_specs = [
        pl.BlockSpec((256, RX * CH), lambda g: (0, 0)),
        pl.BlockSpec((RX * CH, 512), lambda g: (0, g)),
        pl.BlockSpec((1, RYP, 512), lambda g: (g, 0, 0)),
        pl.BlockSpec((256, RYP), lambda g: (0, 0)),
        pl.BlockSpec((256, 512), lambda g: (0, g)),
        pl.BlockSpec((CH, HID), lambda g: (0, 0)),
        pl.BlockSpec((HID, CH), lambda g: (0, 0)),
    ]
    args = [yx, kron, yy, c["cyt"], state, we, wr]
    out_specs = [pl.BlockSpec((256, 512), lambda g: (0, g))]
    out_shape = [jax.ShapeDtypeStruct((256, 4096), BF16)]
    scratch = [pltpu.VMEM((256, 1024), BF16), pltpu.VMEM((1024, 256), BF16)]
    if more:
        in_specs.append(pl.BlockSpec((RYP, 256), lambda g: (0, 0)))
        args.append(c["cy"])
        out_specs += [
            pl.BlockSpec((256, RX * CH), lambda g: (0, 0)),
            pl.BlockSpec((1, RYP, 512), lambda g: (g, 0, 0)),
        ]
        out_shape += [
            jax.ShapeDtypeStruct((256, RX * CH), BF16),
            jax.ShapeDtypeStruct((8, RYP, 512), BF16),
        ]
        scratch.append(pltpu.VMEM((256, RX * CH), F32))
    return pl.pallas_call(
        functools.partial(last_kernel, more),
        name="last",
        grid=(8,),
        in_specs=in_specs,
        out_specs=out_specs,
        out_shape=out_shape,
        scratch_shapes=scratch,
        compiler_params=pltpu.CompilerParams(vmem_limit_bytes=48 << 20),
    )(*args)


def gather_weights(spectral_x, spectral_y):
    core = lax.rem(lax.axis_index("gx"), 2)
    swap = [(i, i ^ 1) for i in range(32)]
    same_core = [list(range(c, 32, 2)) for c in range(2)]
    own = jnp.concatenate([spectral_x[:, :, 0], spectral_x[:, :, 1]], axis=-1)
    own = jnp.broadcast_to(own[None], (16, LAYERS, 1, CH, 128))
    wx = lax.all_to_all(own, "gx", 0, 0, axis_index_groups=same_core, tiled=True)
    own = lax.dynamic_slice_in_dim(spectral_y, core * 2, 2, 1)
    own = jnp.concatenate([own[:, :, 0], own[:, :, 1]], axis=-1)
    own = jnp.broadcast_to(own[None], (8, LAYERS, 2, CH, 128))
    wy = lax.all_to_all(own, "gy", 0, 0, tiled=True)
    wx = (wx, lax.ppermute(wx, "gx", swap))
    wy = (wy, lax.ppermute(wy, "gx", swap))
    return wx, wy, core.reshape(1).astype(jnp.int32)


def body(state_field, spectral_x, spectral_y, expand_weight, reduce_weight):
    c = {name: jnp.asarray(value) for name, value in make_constants().items()}
    wx, wy, core = gather_weights(spectral_x, spectral_y)
    state = jnp.transpose(state_field[0], (2, 1, 0)).reshape(256, 4096)
    kron, zx, zy = first_call(state, c)
    for l in range(LAYERS):
        recv_x = lax.all_to_all(zx.reshape(32, LINE, RX * CH), "gx", 0, 0, tiled=True)
        recv_y = lax.all_to_all(zy, "gy", 0, 0, tiled=True)
        send_x = mid_x(core, recv_x, wx, c, l)
        send_y = mid_y(core, recv_y, wy, c, l)
        yx = lax.all_to_all(send_x, "gx", 0, 0, tiled=True).reshape(256, RX * CH)
        yy = lax.all_to_all(send_y, "gy", 0, 0, tiled=True)
        more = l + 1 < LAYERS
        got = last_call(more, yx, kron, yy, state, expand_weight[l], reduce_weight[l], c)
        state = got[0]
        if more:
            zx, zy = got[1], got[2]
    return jnp.transpose(state.reshape(256, 64, CH), (2, 1, 0))[None]


def solution(mesh):
    in_specs = (
        P(None, None, "gx", "gy"),
        P(None, "gx", None, None, None),
        P(None, "gy", None, None, None),
        P(),
        P(),
    )
    out_specs = P(None, None, "gx", "gy")
    return jax.shard_map(body, mesh=mesh, in_specs=in_specs, out_specs=out_specs, check_vma=False)
```

time: 545 us -> 222 us (0.41)
  waiting for transfers between devices: 404 us -> 63.4 us
  matrix products: 51.9 us -> 0 us
  starting transfers between devices: 0.43 us -> 45.3 us
  Pallas kernels: 0 us -> 43.6 us
  blocking collectives: 48.2 us -> 33.2 us
  between operations: 13.8 us -> 0.28 us
  local copies, waits for them, and re-layouts: 20.5 us -> 33.9 us
    reduce_scatter x2 -> x0, waiting for transfers between devices: 217 us -> none  [body(): lax.psum_scatter(jnp.einsum('kx,zcxy->kzcy', forward_xloc, state, preferr...]
    all_gather x2 -> x0, waiting for transfers between devices: 116 us -> none  [body(): lax.all_gather(mixed_x, 'gx', axis=0, tiled=True)]
    unnamed x8 -> x0, waiting for transfers between devices: 70.6 us -> none
    all_to_all x0 -> x8, waiting for transfers between devices: none -> 62 us  [the longest x2 24.9 us: body(): yx = lax.all_to_all(send_x, 'gx', 0, 0, tiled=True).reshape(256, RX * CH)]
    dot_general x26 -> x0, matrix products: 51.9 us -> none  [the longest x2 23 us: body(): jnp.einsum('hc,zhxy->zcxy', reduce_weight[layer_index], hidden, preferred...]
    all_gather x2 -> x0, blocking collectives: 48.2 us -> none  [body(): lax.all_gather(mixed_y, 'gy', axis=0, tiled=True)]
    all_to_all x0 -> x8, starting transfers between devices: none -> 44.7 us  [the longest x2 14.9 us: body(): lax.all_to_all(zx.reshape(32, LINE, RX * CH), 'gx', 0, 0, tiled=True)]
    pallas_call x0 -> x7, Pallas kernels: none -> 43.6 us  [the longest x2 27.7 us: last_call(): pl.pallas_call(functools.partial(last_kernel, more), name='last', grid=(8...]
  transfers between devices with their start and end apart: 6 -> 10, of which waited for: 6 -> 9; matrix products, arithmetic and copies ran while one was open for 5% -> 2% of each run, Pallas kernels for 0% -> 4%
where the time goes in v1:
time: 222 us; the launch traced here: 220 us
  waiting for transfers between devices  63.4 us (29%)
  starting transfers between devices  45.3 us (20%)
  Pallas kernels  43.6 us (20%)
  local copies, waits for them, and re-layouts  33.9 us (15%)
  blocking collectives  33.2 us (15%)
    pallas_call x2, Pallas kernels, last_call(): pl.pallas_call(functools.partial(last_kernel, more), name='last', grid=(8...  27.7 us
    all_to_all x2, waiting for transfers between devices, body(): yx = lax.all_to_all(send_x, 'gx', 0, 0, tiled=True).reshape(256, RX * CH)  24.9 us
    all_to_all x1, blocking collectives, gather_weights(): lax.all_to_all(own, 'gx', 0, 0, axis_index_groups=same_core, tiled=True)  24.8 us
    unnamed x59, local copies, waits for them, and re-layouts  20.6 us
    all_to_all x2, waiting for transfers between devices, body(): lax.all_to_all(zx.reshape(32, LINE, RX * CH), 'gx', 0, 0, tiled=True)  17.5 us
    all_to_all x2, starting transfers between devices, body(): lax.all_to_all(zx.reshape(32, LINE, RX * CH), 'gx', 0, 0, tiled=True)  14.9 us
    all_to_all x2, starting transfers between devices, body(): yx = lax.all_to_all(send_x, 'gx', 0, 0, tiled=True).reshape(256, RX * CH)  13.1 us
    all_to_all x1, waiting for transfers between devices, gather_weights(): wy = lax.all_to_all(own, 'gy', 0, 0, tiled=True)  9.38 us
  transfers between devices with their start and end apart: 10, of which 9 were waited for; matrix products, arithmetic and copies ran while one was open for 2% of the time, Pallas kernels for 4%

profile of v1, /device:TPU:1, one launch (start us, length us, event | category | flops | bytes accessed | tf_op | source)
XLA Modules:
  0.0 219.9 jit_solution(14105003211171953991)
XLA Ops:
  0.0 4.1 %copy.19 = bf16[1,64,64,256]{3,1,2,0:T(8,128)(2,1)} copy(bf16[1,64,64,256]{3,2,1,0:T(8,128)(2,1)} %param.12) | data formatting | bytes 4194304 | tf_op args[0]
  4.1 2.9 %copy.20.state_ref.refs_4_ = bf16[256,4096]{1,0:T(8,128)(2,1)S(1)} copy(bf16[256,4096]{0,1:T(8,128)(2,1)} %bitcast.42) | data formatting | bytes 4194304 | tf_op jit(solution)/shard_map/reshape | solution.py:353
  7.1 0.0 copy-start.26
  7.1 0.0 copy-start.27
  7.1 7.3 %first.1 = (bf16[640,4096]{1,0:T(8,128)(2,1)}, bf16[256,640]{1,0:T(8,128)(2,1)S(1)}, bf16[8,24,512]{2,1,0:T(8,128)(2,1)}) custom-call(bf16[256,4096]{1,0:T(8,128)(2,1)S(1)} %copy.20.state_ref.refs_4_, bf16[16,4096]{1,0:T(8,128)(2,1)S(1)} %copy-done.20, bf16[24,256]{1,0:T(8,128)(2,1)S(1)} %copy-done.23), custom_call_target="tpu_custom_call" | custom-call | tf_op jit(solution)/shard_map/first/pallas_call | solution.py:106
  14.4 0.7 copy-done.9
  15.1 5.8 %all-to-all-start.3 = ((bf16[8,24,512]{2,1,0:T(8,128)(2,1)}), bf16[8,24,512]{2,1,0:T(8,128)(2,1)S(1)}, u32[]{:S(2)}, u32[]{:S(2)}) async-start(bf16[8,24,512]{2,1,0:T(8,128)(2,1)} %get-tuple-element.13), calls=%async_computation.3 | async-start | bytes 393216 | tf_op jit(solution)/shard_map/all_to_all | solution.py:357
  21.0 0.1 pad_maximum_fusion
  21.1 6.0 %all-to-all-done.3.recv_ref = bf16[8,24,512]{2,1,0:T(8,128)(2,1)S(1)} async-done(((bf16[8,24,512]{2,1,0:T(8,128)(2,1)}), bf16[8,24,512]{2,1,0:T(8,128)(2,1)S(1)}, u32[]{:S(2)}, u32[]{:S(2)}) %all-to-all-start.3) | async-done | bytes 196640 | tf_op jit(solution)/shard_map/all_to_all | solution.py:357
  27.0 0.9 broadcast_in_dim.19
  28.0 3.5 %all-to-all-start.4 = ((bf16[8,2,2,64,128]{4,3,2,1,0:T(8,128)(2,1)}), bf16[8,2,2,64,128]{4,3,2,1,0:T(8,128)(2,1)S(1)}, u32[]{:S(2)}, u32[]{:S(2)}) async-start(bf16[8,2,2,64,128]{4,3,2,1,0:T(8,128)(2,1)} %broadcast_in_dim.19), calls=%async_computation.4 | async-start | bytes 1048576 | tf_op jit(solution)/shard_map/all_to_all | solution.py:344
  31.5 0.1 maximum_bitcast_fusion
  31.6 0.0 copy-start.8
  31.6 9.4 %all-to-all-done.4.w0_ref = bf16[8,2,2,64,128]{4,3,2,1,0:T(8,128)(2,1)S(1)} async-done(((bf16[8,2,2,64,128]{4,3,2,1,0:T(8,128)(2,1)}), bf16[8,2,2,64,128]{4,3,2,1,0:T(8,128)(2,1)S(1)}, u32[]{:S(2)}, u32[]{:S(2)}) %all-to-all-start.4) | async-done | bytes 524320 | tf_op jit(solution)/shard_map/all_to_all | solution.py:344
  41.0 0.1 broadcast_in_dim.18
  41.1 24.8 %all_to_all.50.w0_ref = bf16[16,2,1,64,128]{4,3,2,1,0:T(8,128)(2,1)S(1)} all-to-all(bf16[16,2,1,64,128]{4,3,2,1,0:T(8,128)(2,1)S(1)} %broadcast_in_dim.18), channel_id=1, replica_groups={{0,16,32,48,64,80,96,112,128,144,160,176,192,208,224,240},{8,24,40,56,7..., dimensions={0} | all-to-all | bytes 1048576 | tf_op jit(solution)/shard_map/all_to_all | solution.py:340
  65.9 8.3 %all-to-all-start = ((bf16[32,8,640]{2,1,0:T(8,128)(2,1)}), bf16[32,8,640]{2,1,0:T(8,128)(2,1)S(1)}, u32[]{:S(2)}, u32[]{:S(2)}) async-start(bf16[32,8,640]{2,1,0:T(8,128)(2,1)} %bitcast.37), calls=%async_computation | async-start | bytes 655360 | tf_op jit(solution)/shard_map/all_to_all | solution.py:356
  74.3 0.3 collective-permute-start.1
  74.6 0.3 collective-permute-start
  74.9 1.4 collective-permute-done.1.w1_ref
  76.3 0.9 copy-done.6
  77.2 0.8 copy-done.16
  78.0 0.8 copy-done.21
  78.8 1.2 mid_y.2
  80.0 0.8 copy-done.2
  80.8 0.7 copy-done.7
  81.4 7.3 %all-to-all-done.recv_ref = bf16[32,8,640]{2,1,0:T(8,128)(2,1)S(1)} async-done(((bf16[32,8,640]{2,1,0:T(8,128)(2,1)}), bf16[32,8,640]{2,1,0:T(8,128)(2,1)S(1)}, u32[]{:S(2)}, u32[]{:S(2)}) %all-to-all-start) | async-done | bytes 327712 | tf_op jit(solution)/shard_map/all_to_all | solution.py:356
  88.8 4.0 %all-to-all-start.5 = ((bf16[8,24,512]{2,1,0:T(8,128)(2,1)}), bf16[8,24,512]{2,1,0:T(8,128)(2,1)}, u32[]{:S(2)}, u32[]{:S(2)}) async-start(bf16[8,24,512]{2,1,0:T(8,128)(2,1)} %copy-done.7), calls=%async_computation.5 | async-start | bytes 393216 | tf_op jit(solution)/shard_map/all_to_all | solution.py:361
  92.8 0.0 collective-permute-done.w1_ref
  92.8 0.0 copy-start.14
  92.8 0.8 copy-done.14
  93.6 2.4 %mid_x.2 = bf16[32,8,640]{2,1,0:T(8,128)(2,1)S(1)} custom-call(s32[1]{0:T(128)} %bitcast.core_ref, bf16[32,8,640]{2,1,0:T(8,128)(2,1)S(1)} %all-to-all-done.recv_ref, bf16[16,2,1,64,128]{4,3,2,1,0:T(8,128)(2,1)S(1)} %all_to_all.50.w0_ref, bf16[16,2,1,64,128]{4,3,2,1,0:T(8,128)(2,1)} %collective-permute-done.w1_ref, bf16[128,160]{1,0:T(8,128)(2,1)S(1)} %copy-done.14, ...), custom_call_target="tpu_custom_call" | custom-call | tf_op jit(solution)/shard_map/mid_x/pallas_call | solution.py:190
  96.0 0.0 copy-start.4
  96.0 0.7 copy-done.4
  96.8 1.8 all-to-all-done.5.refs_2_
  98.6 6.5 %all-to-all-start.2 = ((bf16[32,8,640]{2,1,0:T(8,128)(2,1)}), bf16[32,8,640]{2,1,0:T(8,128)(2,1)S(1)}, u32[]{:S(2)}, u32[]{:S(2)}) async-start(bf16[32,8,640]{2,1,0:T(8,128)(2,1)} %copy-done.4), calls=%async_computation.2 | async-start | bytes 655360 | tf_op jit(solution)/shard_map/all_to_all | solution.py:360
  105.1 1.4 fusion
  106.5 1.5 copy.30
  107.9 1.4 slice_bitcast_fusion
  109.3 10.4 %all-to-all-done.2 = bf16[32,8,640]{2,1,0:T(8,128)(2,1)S(1)} async-done(((bf16[32,8,640]{2,1,0:T(8,128)(2,1)}), bf16[32,8,640]{2,1,0:T(8,128)(2,1)S(1)}, u32[]{:S(2)}, u32[]{:S(2)}) %all-to-all-start.2) | async-done | bytes 327712 | tf_op jit(solution)/shard_map/all_to_all | solution.py:360
  119.7 0.8 copy-done.11
  120.5 0.8 copy-done.13
  121.4 0.8 copy-done.19
  122.1 0.7 copy-done.24
  122.8 16.0 %last.2 = (bf16[256,4096]{1,0:T(8,128)(2,1)S(1)}, bf16[256,640]{1,0:T(8,128)(2,1)S(1)}, bf16[8,24,512]{2,1,0:T(8,128)(2,1)S(1)}) custom-call(bf16[256,640]{1,0:T(8,128)(2,1)S(1)} %bitcast.35, bf16[640,4096]{1,0:T(8,128)(2,1)} %get-tuple-element.12.refs_1_, bf16[8,24,512]{2,1,0:T(8,128)(2,1)} %all-to-all-done.5.refs_2_, bf16[256,24]{1,0:T(8,128)(2,1)S(1)} %copy-done.11, ...), custom_call_target="tpu_custom_call" | custom-call | tf_op jit(solution)/shard_map/last/pallas_call | solution.py:322
  138.9 0.0 copy-start
  138.9 1.3 copy-done
  140.2 8.3 %all_to_all.51.recv_ref = bf16[8,24,512]{2,1,0:T(8,128)(2,1)S(1)} all-to-all(bf16[8,24,512]{2,1,0:T(8,128)(2,1)S(1)} %get-tuple-element.15), channel_id=1, replica_groups=mesh['gx'=32,'gy'=8] {'gy'}, dimensions={0} | all-to-all | bytes 393216 | tf_op jit(solution)/shard_map/all_to_all | solution.py:357
  148.5 6.6 %all-to-all-start.6 = ((bf16[32,8,640]{2,1,0:T(8,128)(2,1)}), bf16[32,8,640]{2,1,0:T(8,128)(2,1)S(1)}, u32[]{:S(2)}, u32[]{:S(2)}) async-start(bf16[32,8,640]{2,1,0:T(8,128)(2,1)} %bitcast.38), calls=%async_computation.6 | async-start | bytes 655360 | tf_op jit(solution)/shard_map/all_to_all | solution.py:356
  155.1 1.0 copy-done.3
  156.1 0.8 copy-done.17
  156.9 0.8 copy-done.22
  157.7 1.9 mid_y.3
  159.6 10.1 %all-to-all-done.6.recv_ref = bf16[32,8,640]{2,1,0:T(8,128)(2,1)S(1)} async-done(((bf16[32,8,640]{2,1,0:T(8,128)(2,1)}), bf16[32,8,640]{2,1,0:T(8,128)(2,1)S(1)}, u32[]{:S(2)}, u32[]{:S(2)}) %all-to-all-start.6) | async-done | bytes 327712 | tf_op jit(solution)/shard_map/all_to_all | solution.py:356
  169.7 3.4 %all-to-all-start.9 = ((bf16[8,24,512]{2,1,0:T(8,128)(2,1)}), bf16[8,24,512]{2,1,0:T(8,128)(2,1)S(1)}, u32[]{:S(2)}, u32[]{:S(2)}) async-start(bf16[8,24,512]{2,1,0:T(8,128)(2,1)} %mid_y.3), calls=%async_computation.9 | async-start | bytes 393216 | tf_op jit(solution)/shard_map/all_to_all | solution.py:361
  173.1 3.1 %mid_x.3 = bf16[32,8,640]{2,1,0:T(8,128)(2,1)} custom-call(s32[1]{0:T(128)} %bitcast.core_ref, bf16[32,8,640]{2,1,0:T(8,128)(2,1)S(1)} %all-to-all-done.6.recv_ref, bf16[16,2,1,64,128]{4,3,2,1,0:T(8,128)(2,1)S(1)} %all_to_all.50.w0_ref, bf16[16,2,1,64,128]{4,3,2,1,0:T(8,128)(2,1)} %collective-permute-done.w1_ref, bf16[128,160]{1,0:T(8,128)(2,1)S(1)} %copy-done.15, ...), custom_call_target="tpu_custom_call" | custom-call | tf_op jit(solution)/shard_map/mid_x/pallas_call | solution.py:190
  176.3 2.6 %all-to-all-done.9.refs_2_ = bf16[8,24,512]{2,1,0:T(8,128)(2,1)S(1)} async-done(((bf16[8,24,512]{2,1,0:T(8,128)(2,1)}), bf16[8,24,512]{2,1,0:T(8,128)(2,1)S(1)}, u32[]{:S(2)}, u32[]{:S(2)}) %all-to-all-start.9) | async-done | bytes 196640 | tf_op jit(solution)/shard_map/all_to_all | solution.py:361
  178.8 6.6 %all-to-all-start.7 = ((bf16[32,8,640]{2,1,0:T(8,128)(2,1)}), bf16[32,8,640]{2,1,0:T(8,128)(2,1)S(1)}, u32[]{:S(2)}, u32[]{:S(2)}) async-start(bf16[32,8,640]{2,1,0:T(8,128)(2,1)} %mid_x.3), calls=%async_computation.7 | async-start | bytes 655360 | tf_op jit(solution)/shard_map/all_to_all | solution.py:360
  185.5 0.1 copy.31
  185.6 14.5 %all-to-all-done.7 = bf16[32,8,640]{2,1,0:T(8,128)(2,1)S(1)} async-done(((bf16[32,8,640]{2,1,0:T(8,128)(2,1)}), bf16[32,8,640]{2,1,0:T(8,128)(2,1)S(1)}, u32[]{:S(2)}, u32[]{:S(2)}) %all-to-all-start.7) | async-done | bytes 327712 | tf_op jit(solution)/shard_map/all_to_all | solution.py:360
  200.1 1.6 copy-done.1
  201.7 11.6 %last.3 = bf16[256,4096]{1,0:T(8,128)(2,1)S(1)} custom-call(bf16[256,640]{1,0:T(8,128)(2,1)S(1)} %bitcast.36, bf16[640,4096]{1,0:T(8,128)(2,1)} %get-tuple-element.12.refs_1_, bf16[8,24,512]{2,1,0:T(8,128)(2,1)S(1)} %all-to-all-done.9.refs_2_, bf16[256,24]{1,0:T(8,128)(2,1)S(1)} %copy-done.12, bf16[256,4096]{1,0:T(8,128)(2,1)S(1)} %copy-done.1, ...), custom_call_target="tpu_custom_call" | custom-call | tf_op jit(solution)/shard_map/last/pallas_call | solution.py:322
  213.3 2.5 %copy.26 = bf16[256,4096]{0,1:T(8,128)(2,1)} copy(bf16[256,4096]{1,0:T(8,128)(2,1)S(1)} %last.3) | data formatting | bytes 4194304 | tf_op jit(solution)/shard_map/last/pallas_call | solution.py:322
  215.8 4.1 %copy.27 = bf16[1,64,64,256]{3,2,1,0:T(8,128)(2,1)} copy(bf16[1,64,64,256]{3,1,2,0:T(8,128)(2,1)} %bitcast.41) | data formatting | bytes 4194304 | tf_op jit(solution)/shard_map/broadcast_in_dim | solution.py:367
  (35 shorter events, 0.1 us)
Async XLA Ops:
  4.1 3.0 %copy-start.20 = (bf16[16,4096]{1,0:T(8,128)(2,1)S(1)}, bf16[16,4096]{1,0:T(8,128)(2,1)}, u32[]{:S(2)}) copy-start(bf16[16,4096]{1,0:T(8,128)(2,1)} %constant.35.clone.bexp_ref) | copy-start | bytes 393220
  4.1 3.0 %copy-start.23 = (bf16[24,256]{1,0:T(8,128)(2,1)S(1)}, bf16[24,256]{1,0:T(8,128)(2,1)}, u32[]{:S(2)}) copy-start(bf16[24,256]{1,0:T(8,128)(2,1)} %constant.33.clone.cy_ref.refs_7_) | copy-start | bytes 36868
  7.1 13.9 %copy-start.26 = (bf16[2,4,2,64,64]{4,3,2,1,0:T(8,128)(2,1)S(1)}, bf16[2,4,2,64,64]{4,3,2,1,0:T(8,128)(2,1)}, u32[]{:S(2)}) copy-start(bf16[2,4,2,64,64]{4,3,2,1,0:T(8,128)(2,1)} %param.14) | copy-start | bytes 393220
  7.1 24.4 %copy-start.27 = (bf16[2,1,2,64,64]{4,3,2,1,0:T(8,128)(2,1)S(1)}, bf16[2,1,2,64,64]{4,3,2,1,0:T(8,128)(2,1)}, u32[]{:S(2)}) copy-start(bf16[2,1,2,64,64]{4,3,2,1,0:T(8,128)(2,1)} %param.13) | copy-start | bytes 98308
  14.4 0.7 copy-start.9
  15.1 11.9 %all-to-all-start.3 = ((bf16[8,24,512]{2,1,0:T(8,128)(2,1)}), bf16[8,24,512]{2,1,0:T(8,128)(2,1)S(1)}, u32[]{:S(2)}, u32[]{:S(2)}) async-start(bf16[8,24,512]{2,1,0:T(8,128)(2,1)} %get-tuple-element.13), calls=%async_computation.3 | async-start | bytes 393216 | tf_op jit(solution)/shard_map/all_to_all | solution.py:357
  27.0 0.9 copy-start.5
  28.0 13.0 %all-to-all-start.4 = ((bf16[8,2,2,64,128]{4,3,2,1,0:T(8,128)(2,1)}), bf16[8,2,2,64,128]{4,3,2,1,0:T(8,128)(2,1)S(1)}, u32[]{:S(2)}, u32[]{:S(2)}) async-start(bf16[8,2,2,64,128]{4,3,2,1,0:T(8,128)(2,1)} %broadcast_in_dim.19), calls=%async_computation.4 | async-start | bytes 1048576 | tf_op jit(solution)/shard_map/all_to_all | solution.py:344
  31.6 61.2 %copy-start.8 = (bf16[320,64]{1,0:T(8,128)(2,1)S(1)}, bf16[320,64]{1,0:T(8,128)(2,1)}, u32[]{:S(2)}) copy-start(bf16[320,64]{1,0:T(8,128)(2,1)} %constant.30.clone.ux_ref) | copy-start | bytes 122884
  65.9 22.8 %all-to-all-start = ((bf16[32,8,640]{2,1,0:T(8,128)(2,1)}), bf16[32,8,640]{2,1,0:T(8,128)(2,1)S(1)}, u32[]{:S(2)}, u32[]{:S(2)}) async-start(bf16[32,8,640]{2,1,0:T(8,128)(2,1)} %bitcast.37), calls=%async_computation | async-start | bytes 655360 | tf_op jit(solution)/shard_map/all_to_all | solution.py:356
  74.3 2.0 collective-permute-start.1
  74.6 18.2 %collective-permute-start = (bf16[16,2,1,64,128]{4,3,2,1,0:T(8,128)(2,1)S(1)}, bf16[16,2,1,64,128]{4,3,2,1,0:T(8,128)(2,1)}, u32[]{:S(2)}, u32[]{:S(2)}) collective-permute-start(bf16[16,2,1,64,128]{4,3,2,1,0:T(8,128)(2,1)S(1)} %all_to_all.50.w0_ref), channel_id=1, source_target_pairs={{0,8},{8,0},{16,24},{24,16},{32,40},{40,32},{48,56},{56,48},{64,72... | collective-permute-start | bytes 1572872 | tf_op jit(solution)/shard_map/ppermute | solution.py:345
  76.3 0.9 copy-start.6
  77.2 0.8 copy-start.16
  78.0 0.8 copy-start.21
  80.0 0.8 copy-start.2
  80.8 0.7 copy-start.7
  88.8 9.8 %all-to-all-start.5 = ((bf16[8,24,512]{2,1,0:T(8,128)(2,1)}), bf16[8,24,512]{2,1,0:T(8,128)(2,1)}, u32[]{:S(2)}, u32[]{:S(2)}) async-start(bf16[8,24,512]{2,1,0:T(8,128)(2,1)} %copy-done.7), calls=%async_computation.5 | async-start | bytes 393216 | tf_op jit(solution)/shard_map/all_to_all | solution.py:361
  92.8 0.8 copy-start.14
  96.0 0.7 copy-start.4
  98.6 21.1 %all-to-all-start.2 = ((bf16[32,8,640]{2,1,0:T(8,128)(2,1)}), bf16[32,8,640]{2,1,0:T(8,128)(2,1)S(1)}, u32[]{:S(2)}, u32[]{:S(2)}) async-start(bf16[32,8,640]{2,1,0:T(8,128)(2,1)} %copy-done.4), calls=%async_computation.2 | async-start | bytes 655360 | tf_op jit(solution)/shard_map/all_to_all | solution.py:360
  119.7 0.8 copy-start.11
  120.5 0.8 copy-start.13
  121.4 0.8 copy-start.19
  122.1 0.7 copy-start.24
  138.9 1.3 copy-start
  140.2 8.3 %copy-start.10 = (bf16[256,640]{1,0:T(8,128)(2,1)}, bf16[256,640]{1,0:T(8,128)(2,1)S(1)}, u32[]{:S(2)}) copy-start(bf16[256,640]{1,0:T(8,128)(2,1)S(1)} %get-tuple-element.14) | copy-start | bytes 983044
  140.2 32.9 %copy-start.15 = (bf16[128,160]{1,0:T(8,128)(2,1)S(1)}, bf16[128,160]{1,0:T(8,128)(2,1)}, u32[]{:S(2)}) copy-start(bf16[128,160]{1,0:T(8,128)(2,1)} %constant.29.clone.ax_ref) | copy-start | bytes 122884
  148.5 21.2 %all-to-all-start.6 = ((bf16[32,8,640]{2,1,0:T(8,128)(2,1)}), bf16[32,8,640]{2,1,0:T(8,128)(2,1)S(1)}, u32[]{:S(2)}, u32[]{:S(2)}) async-start(bf16[32,8,640]{2,1,0:T(8,128)(2,1)} %bitcast.38), calls=%async_computation.6 | async-start | bytes 655360 | tf_op jit(solution)/shard_map/all_to_all | solution.py:356
  155.1 1.0 copy-start.3
  156.1 0.8 copy-start.17
  156.9 0.8 copy-start.22
  157.7 27.8 %copy-start.25 = (bf16[1,256,64]{1,2,0:T(8,128)(2,1)S(1)}, bf16[1,256,64]{1,2,0:T(8,128)(2,1)}, u32[]{:S(2)}) copy-start(bf16[1,256,64]{1,2,0:T(8,128)(2,1)} %get-tuple-element.19) | copy-start | bytes 98308
  157.7 42.4 %copy-start.12 = (bf16[256,24]{1,0:T(8,128)(2,1)S(1)}, bf16[256,24]{1,0:T(8,128)(2,1)}, u32[]{:S(2)}) copy-start(bf16[256,24]{1,0:T(8,128)(2,1)} %constant.34.clone.refs_3_) | copy-start | bytes 36868
  157.7 42.4 %copy-start.18 = (bf16[64,256]{1,0:T(8,128)(2,1)S(1)}, bf16[64,256]{1,0:T(8,128)(2,1)}, u32[]{:S(2)}) copy-start(bf16[64,256]{1,0:T(8,128)(2,1)} %get-tuple-element.21.refs_5_) | copy-start | bytes 98308
  169.7 9.1 %all-to-all-start.9 = ((bf16[8,24,512]{2,1,0:T(8,128)(2,1)}), bf16[8,24,512]{2,1,0:T(8,128)(2,1)S(1)}, u32[]{:S(2)}, u32[]{:S(2)}) async-start(bf16[8,24,512]{2,1,0:T(8,128)(2,1)} %mid_y.3), calls=%async_computation.9 | async-start | bytes 393216 | tf_op jit(solution)/shard_map/all_to_all | solution.py:361
  178.8 21.3 %all-to-all-start.7 = ((bf16[32,8,640]{2,1,0:T(8,128)(2,1)}), bf16[32,8,640]{2,1,0:T(8,128)(2,1)S(1)}, u32[]{:S(2)}, u32[]{:S(2)}) async-start(bf16[32,8,640]{2,1,0:T(8,128)(2,1)} %mid_x.3), calls=%async_computation.7 | async-start | bytes 655360 | tf_op jit(solution)/shard_map/all_to_all | solution.py:360
  200.1 1.6 copy-start.1

commit v2 on v1

v2 whole, which is shorter than its diff:
```python
import functools

import jax
import jax.numpy as jnp
import numpy as np
from jax import lax
from jax.experimental import pallas as pl
from jax.experimental.pallas import tpu as pltpu
from jax.sharding import PartitionSpec as P

F32 = jnp.float32
BF16 = jnp.bfloat16
NX = 2048
NY = 2048
CH = 64
HID = 256
MODES = 32
LAYERS = 2
RX = 10
RY = 20
RYP = 24
LINE = 8


def window_tables(length, devices, rank):
    window = length // devices
    k = np.arange(MODES)[:, None]
    p = np.arange(length)[None, :]
    angle = 2.0 * np.pi * ((k * p) % length) / length
    scale = 1.0 / np.sqrt(length)
    weight = np.where(np.arange(MODES) == 0, 1.0, 2.0)[:, None]
    forward = np.concatenate([np.cos(angle), -np.sin(angle)], 0) * scale
    inverse = np.concatenate([weight * np.cos(angle), -weight * np.sin(angle)], 0) * scale
    _, _, vt = np.linalg.svd(forward[:, :window], full_matrices=False)
    basis = vt[:rank]
    basis = basis * np.sign(basis[np.arange(rank), np.abs(basis).argmax(1)])[:, None]
    fwd = np.stack([forward[:, d * window : (d + 1) * window] @ basis.T for d in range(devices)])
    inv = np.stack([inverse[:, d * window : (d + 1) * window] @ basis.T for d in range(devices)])
    return basis, fwd, inv


def bf(x):
    return np.asarray(x, np.float32).astype(jnp.bfloat16)


def make_constants():
    bx, fx, ix = window_tables(NX, 32, RX)
    by, fy, iy = window_tables(NY, 8, RY)
    pairs = RX // 2
    ax = fx.reshape(32, 64, pairs, 2).transpose(3, 1, 2, 0).reshape(128, pairs * 32)
    gx = ix.reshape(32, 2, MODES, pairs, 2)
    u0 = gx[..., 0].transpose(3, 0, 1, 2).reshape(pairs * 32, 64)
    u1 = gx[..., 1].transpose(3, 0, 1, 2)[:, :, ::-1].reshape(pairs * 32, 64)
    mid_x = np.zeros((448, 256))
    mid_x[:128, : pairs * 32] = ax
    mid_x[128:, :64] = np.concatenate([u0, u1], 0)
    pad = ((0, 0), (0, 0), (0, RYP - RY))
    fy, iy = np.pad(fy, pad), np.pad(iy, pad)
    mid_y = np.zeros((8, 96, 256))
    for me in range(8):
        order = [(me - s) % 8 for s in range(8)]
        mid_y[me, :64, : 8 * RYP] = fy[order].transpose(1, 0, 2).reshape(64, 8 * RYP)
        mid_y[me, 64 : 64 + RYP, :64] = iy[me].T
    cy = np.pad(by, ((0, RYP - RY), (0, 0)))
    bexp = np.repeat(bx, CH, axis=1)
    bexp = np.pad(bexp, ((0, 16 - RX), (0, 0)))
    return dict(mid_x=bf(mid_x), mid_y=bf(mid_y), cy=bf(cy), bexp=bf(bexp))


def dot(a, b):
    return jnp.dot(a, b, preferred_element_type=F32)


def dot_nt(a, b):
    return lax.dot_general(a, b, (((1,), (1,)), ((), ())), preferred_element_type=F32)


def half_mask(rows):
    return lax.broadcasted_iota(jnp.int32, (rows, 128), 1) < 64


def dot_tn(a, b):
    return lax.dot_general(a, b, (((0,), (0,)), ((), ())), preferred_element_type=F32)


def estimate(us):
    return pl.CostEstimate(flops=int(us * 1e9), bytes_accessed=1 << 20, transcendentals=0)


def params():
    return pltpu.CompilerParams(vmem_limit_bytes=48 << 20)


def first_kernel(field_ref, bexp_ref, cy_ref, kron_ref, state_ref, zx_ref, zy_ref, t_ref, acc_ref):
    g = pl.program_id(0)
    for h in range(2):
        part = field_ref[:, :, h * 128 : (h + 1) * 128].astype(F32)
        t_ref[h] = part.reshape(512, 128)
    for h in range(2):
        for p in range(4):
            two = [t_ref[h, pl.ds(2 * p + j, CH, stride=8), :] for j in range(2)]
            block = jnp.concatenate(two, axis=0).T.astype(BF16)
            state_ref[h * 128 : (h + 1) * 128, p * 128 : (p + 1) * 128] = block
    lanes = lax.broadcasted_iota(jnp.int32, (CH, 512), 1)
    rows = lax.broadcasted_iota(jnp.int32, (CH, 512), 0)
    eye = (lanes % CH) == rows
    for r in range(RX):
        row = jnp.broadcast_to(bexp_ref[r : r + 1, :].astype(F32), (CH, 512))
        kron_ref[r * CH : (r + 1) * CH, :] = jnp.where(eye, row, 0.0).astype(BF16)
    state = state_ref[...]
    part = dot_nt(state, kron_ref[...])

    @pl.when(g == 0)
    def _():
        acc_ref[...] = part

    @pl.when(g > 0)
    def _():
        acc_ref[...] += part

    zy_ref[...] = dot(cy_ref[...], state).astype(BF16)

    @pl.when(g == pl.num_programs(0) - 1)
    def _():
        zx_ref[...] = acc_ref[...].astype(BF16)


def first_call(field, c):
    return pl.pallas_call(
        first_kernel,
        name="first",
        grid=(8,),
        in_specs=[
            pl.BlockSpec((CH, 8, 256), lambda g: (0, g, 0)),
            pl.BlockSpec((16, 512), lambda g: (0, g)),
            pl.BlockSpec((RYP, 256), lambda g: (0, 0)),
        ],
        out_specs=[
            pl.BlockSpec((RX * CH, 512), lambda g: (0, g)),
            pl.BlockSpec((256, 512), lambda g: (0, g)),
            pl.BlockSpec((256, RX * CH), lambda g: (0, 0)),
            pl.BlockSpec((RYP, 512), lambda g: (0, g)),
        ],
        out_shape=[
            jax.ShapeDtypeStruct((RX * CH, 4096), BF16),
            jax.ShapeDtypeStruct((256, 4096), BF16),
            jax.ShapeDtypeStruct((256, RX * CH), BF16),
            jax.ShapeDtypeStruct((RYP, 4096), BF16),
        ],
        scratch_shapes=[pltpu.VMEM((2, 512, 128), F32), pltpu.VMEM((256, RX * CH), F32)],
        compiler_params=params(),
        cost_estimate=estimate(10),
    )(field, c["bexp"], c["cy"])


def mode_weights(w, sign):
    w = w.astype(F32)
    return jnp.concatenate([w * sign, pltpu.roll(w, 64, 1)], axis=0).astype(BF16)


def mix(xs_ref, ms_ref, lines, weights):
    sign = jnp.where(half_mask(CH), 1.0, -1.0)
    for mode, w in weights:
        start = mode * lines
        if not isinstance(start, int):
            start = pl.multiple_of(start, lines)
        rows = pl.ds(start, lines)
        ms_ref[rows, :] = dot_nt(xs_ref[rows, :].astype(BF16), mode_weights(w, sign))


def mid_x_kernel(early, core_ref, recv_ref, w0_ref, w1_ref, tab_ref, *refs):
    send_ref, r_ref, xs_ref, ms_ref, o_ref = refs
    pairs = RX // 2
    first = half_mask(MODES)
    for p in range(pairs):
        part = recv_ref[:, :, p * 128 : (p + 1) * 128]
        r_ref[p] = part.reshape(256, 128).astype(F32)
    cols = []
    for y in range(LINE):
        ry = [r_ref[p, pl.ds(y, 32, stride=LINE), :] for p in range(pairs)]
        cols.append(jnp.concatenate(ry, axis=0).astype(BF16))
    spec = dot(tab_ref[:128, : pairs * 32], jnp.concatenate(cols, axis=1))
    for y in range(LINE):
        s = spec[:, y * 128 : (y + 1) * 128]
        x = jnp.where(first, s[0:32], s[96:128])
        x = x + pltpu.roll(jnp.where(first, s[32:64], s[64:96]), 64, 1)
        xs_ref[pl.ds(y, MODES, stride=LINE), :] = x
    if early:
        core = core_ref[0]
        weights = [(t * 2 + core, w0_ref[t]) for t in range(16)]
        weights += [(t * 2 + 1 - core, w1_ref[t]) for t in range(16)]
    else:
        weights = [(k, w0_ref[k, 0]) for k in range(MODES)]
    mix(xs_ref, ms_ref, LINE, weights)
    cols = []
    for y in range(LINE):
        m = ms_ref[pl.ds(y, MODES, stride=LINE), :]
        cols.append(jnp.concatenate([m, pltpu.roll(m, 64, 1)], axis=0).astype(BF16))
    out = dot(tab_ref[128:, :64], jnp.concatenate(cols, axis=1))
    for y in range(LINE):
        for p in range(pairs):
            v0 = out[p * 32 : (p + 1) * 32, y * 128 : (y + 1) * 128]
            v1 = out[(pairs + p) * 32 : (pairs + p + 1) * 32, y * 128 : (y + 1) * 128]
            o_ref[p, pl.ds(y, 32, stride=LINE), :] = jnp.where(first, v0, v1)
    for p in range(pairs):
        part = o_ref[p].reshape(32, LINE, 128).astype(BF16)
        send_ref[:, :, p * 128 : (p + 1) * 128] = part


def whole(a):
    return pl.BlockSpec(a.shape, lambda *_: (0,) * a.ndim)


def mid_x(early, core, recv, w0, w1, c):
    if early:
        weights = [whole(w0), whole(w1)]
    else:
        weights = [pl.BlockSpec((MODES, 1, CH, 128), lambda i: (0, 1, 0, 0)), whole(w1)]
    return pl.pallas_call(
        functools.partial(mid_x_kernel, early),
        name="mid_x",
        grid=(1,),
        in_specs=[pl.BlockSpec(memory_space=pltpu.SMEM), whole(recv)]
        + weights
        + [whole(c["mid_x"])],
        out_specs=whole(recv),
        out_shape=jax.ShapeDtypeStruct(recv.shape, BF16),
        scratch_shapes=[
            pltpu.VMEM((RX // 2, 256, 128), F32),
            pltpu.VMEM((MODES * LINE, 128), F32),
            pltpu.VMEM((MODES * LINE, 128), F32),
            pltpu.VMEM((RX // 2, 256, 128), F32),
        ],
        compiler_params=params(),
        cost_estimate=estimate(3),
    )(core, recv, w0, w1, c["mid_x"])


def mid_y_kernel(me_ref, *refs):
    z_refs = refs[:8]
    w_ref, tab_ref, out_ref, xs_ref, ms_ref = refs[8:]
    first = half_mask(MODES)
    lines = 64
    for g in range(8):
        z = [ref[:, g * 512 : (g + 1) * 512].astype(F32) for ref in z_refs]
        z = jnp.concatenate(z, axis=0).astype(BF16)
        spec = dot(tab_ref[0, :64, : 8 * RYP], z)
        for b in range(4):
            re = spec[0:32, b * 128 : (b + 1) * 128]
            im = spec[32:64, b * 128 : (b + 1) * 128]
            line = g * 8 + 2 * b
            xs_ref[pl.ds(line, MODES, stride=lines), :] = jnp.where(
                first, re, pltpu.roll(im, 64, 1)
            )
            xs_ref[pl.ds(line + 1, MODES, stride=lines), :] = jnp.where(
                first, pltpu.roll(re, 64, 1), im
            )
    weights = [(src * 4 + j, w_ref[src, 0, j]) for src in range(8) for j in range(4)]
    mix(xs_ref, ms_ref, lines, weights)
    for g in range(8):
        cols = []
        for b in range(4):
            line = g * 8 + 2 * b
            m0 = ms_ref[pl.ds(line, MODES, stride=lines), :]
            m1 = ms_ref[pl.ds(line + 1, MODES, stride=lines), :]
            re = jnp.where(first, m0, pltpu.roll(m1, 64, 1))
            im = jnp.where(first, pltpu.roll(m0, 64, 1), m1)
            cols.append(jnp.concatenate([re, im], axis=0).astype(BF16))
        out = dot(tab_ref[0, 64 : 64 + RYP, :64], jnp.concatenate(cols, axis=1))
        out_ref[g] = out.astype(BF16)


def mid_y(layer, me, zs, w, c):
    table = c["mid_y"]
    return pl.pallas_call(
        mid_y_kernel,
        name="mid_y",
        grid_spec=pltpu.PrefetchScalarGridSpec(
            num_scalar_prefetch=1,
            grid=(1,),
            in_specs=[whole(z) for z in zs]
            + [
                pl.BlockSpec((8, 1, 4, CH, 128), lambda i, me: (0, layer, 0, 0, 0)),
                pl.BlockSpec((1,) + table.shape[1:], lambda i, me: (me[0], 0, 0)),
            ],
            out_specs=pl.BlockSpec((8, RYP, 512), lambda i, me: (0, 0, 0)),
            scratch_shapes=[pltpu.VMEM((MODES * 64, 128), F32)] * 2,
        ),
        out_shape=jax.ShapeDtypeStruct((8, RYP, 512), BF16),
        compiler_params=params(),
        cost_estimate=estimate(6),
    )(me, *zs, w, table)


def gelu(x):
    x = x.astype(BF16)
    inner = x * (0.7978845608028654 + 0.035677408136300125 * (x * x))
    half = 0.5 * x
    return half + half * jnp.tanh(inner)


def last_kernel(more, *refs):
    yx_ref, kron_ref, yy_ref, cy_ref, state_ref, we_ref, wr_ref = refs[:7]
    if more:
        out_ref, zx_ref, zy_ref, we4_ref, wr4_ref, acc_ref = refs[7:]
    else:
        out_ref, we4_ref, wr4_ref, t_ref = refs[7:]
    g = pl.program_id(0)

    @pl.when(g == 0)
    def _():
        we4_ref[...] = jnp.zeros_like(we4_ref)
        wr4_ref[...] = jnp.zeros_like(wr4_ref)
        for j in range(4):
            we4_ref[j * CH : (j + 1) * CH, j * HID : (j + 1) * HID] = we_ref[0]
            wr4_ref[j * CH : (j + 1) * CH, j * HID : (j + 1) * HID] = wr_ref[0]

    kron = kron_ref[...]
    total = dot(yx_ref[...], kron) + dot_tn(cy_ref[...], yy_ref[0])
    total = total.astype(BF16)
    for j in range(2):
        part = total[:, j * 256 : (j + 1) * 256]
        hidden = gelu(dot(part, we4_ref[...])).astype(BF16)
        update = dot_nt(hidden, wr4_ref[...])
        new = state_ref[:, j * 256 : (j + 1) * 256].astype(F32) + update
        if more:
            out_ref[:, j * 256 : (j + 1) * 256] = new.astype(BF16)
            continue
        for h in range(2):
            for p in range(2):
                block = new[h * 128 : (h + 1) * 128, p * 128 : (p + 1) * 128].T
                x = j * 4 + p * 2
                t_ref[h, pl.ds(x, CH, stride=8), :] = block[:CH]
                t_ref[h, pl.ds(x + 1, CH, stride=8), :] = block[CH:]
    if more:
        state = out_ref[...]
        part = dot_nt(state, kron)

        @pl.when(g == 0)
        def _():
            acc_ref[...] = part

        @pl.when(g > 0)
        def _():
            acc_ref[...] += part

        zy_ref[...] = dot(cy_ref[...], state).astype(BF16)

        @pl.when(g == pl.num_programs(0) - 1)
        def _():
            zx_ref[...] = acc_ref[...].astype(BF16)
    else:
        for h in range(2):
            part = t_ref[h].reshape(CH, 8, 128).astype(BF16)
            out_ref[:, :, h * 128 : (h + 1) * 128] = part


def last_call(layer, more, yx, kron, yy, state, we, wr, c):
    in_specs = [
        pl.BlockSpec((256, RX * CH), lambda g: (0, 0)),
        pl.BlockSpec((RX * CH, 512), lambda g: (0, g)),
        pl.BlockSpec((1, RYP, 512), lambda g: (g, 0, 0)),
        pl.BlockSpec((RYP, 256), lambda g: (0, 0)),
        pl.BlockSpec((256, 512), lambda g: (0, g)),
        pl.BlockSpec((1, CH, HID), lambda g: (layer, 0, 0)),
        pl.BlockSpec((1, CH, HID), lambda g: (layer, 0, 0)),
    ]
    scratch = [pltpu.VMEM((256, 1024), BF16)] * 2
    if more:
        out_specs = [
            pl.BlockSpec((256, 512), lambda g: (0, g)),
            pl.BlockSpec((256, RX * CH), lambda g: (0, 0)),
            pl.BlockSpec((RYP, 512), lambda g: (0, g)),
        ]
        out_shape = [
            jax.ShapeDtypeStruct((256, 4096), BF16),
            jax.ShapeDtypeStruct((256, RX * CH), BF16),
            jax.ShapeDtypeStruct((RYP, 4096), BF16),
        ]
        scratch.append(pltpu.VMEM((256, RX * CH), F32))
    else:
        out_specs = [pl.BlockSpec((CH, 8, 256), lambda g: (0, g, 0))]
        out_shape = [jax.ShapeDtypeStruct((CH, 64, 256), BF16)]
        scratch.append(pltpu.VMEM((2, 512, 128), F32))
    return pl.pallas_call(
        functools.partial(last_kernel, more),
        name="last",
        grid=(8,),
        in_specs=in_specs,
        out_specs=out_specs,
        out_shape=out_shape,
        scratch_shapes=scratch,
        compiler_params=params(),
        cost_estimate=estimate(12),
    )(yx, kron, yy, c["cy"], state, we, wr)


def join(w):
    return jnp.concatenate([w[..., 0, :, :], w[..., 1, :, :]], axis=-1)


def body(state_field, spectral_x, spectral_y, expand_weight, reduce_weight):
    c = {name: jnp.asarray(value) for name, value in make_constants().items()}
    core = lax.rem(lax.axis_index("gx"), 2).reshape(1).astype(jnp.int32)
    me = lax.axis_index("gy").reshape(1).astype(jnp.int32)
    own_x = join(spectral_x)[:, 0]
    same_core = [list(range(s, 32, 2)) for s in range(2)]
    early = jnp.broadcast_to(own_x[0][None], (16, CH, 128))
    early = lax.all_to_all(early, "gx", 0, 0, axis_index_groups=same_core, tiled=True)
    swapped = lax.ppermute(early, "gx", [(i, i ^ 1) for i in range(32)])
    wy = lax.all_gather(join(spectral_y), "gy", axis=0)
    wx = lax.all_gather(own_x, "gx", axis=0)
    wr = jnp.swapaxes(reduce_weight, 1, 2)
    kron, state, zx, zy = first_call(state_field[0], c)
    for l in range(LAYERS):
        zs = [zy]
        for s in range(1, 8):
            zs.append(lax.ppermute(zy, "gy", [(i, (i + s) % 8) for i in range(8)]))
        recv = lax.all_to_all(zx.reshape(32, LINE, RX * CH), "gx", 0, 0, tiled=True)
        if l == 0:
            send = mid_x(True, core, recv, early, swapped, c)
        else:
            send = mid_x(False, core, recv, wx, core, c)
        yy = mid_y(l, me, zs, wy, c)
        yx = lax.all_to_all(send, "gx", 0, 0, tiled=True).reshape(256, RX * CH)
        more = l + 1 < LAYERS
        got = last_call(l, more, yx, kron, yy, state, expand_weight, wr, c)
        if more:
            state, zx, zy = got
    return got[0][None]


def solution(mesh):
    in_specs = (
        P(None, None, "gx", "gy"),
        P(None, "gx", None, None, None),
        P(None, "gy", None, None, None),
        P(),
        P(),
    )
    out_specs = P(None, None, "gx", "gy")
    return jax.shard_map(body, mesh=mesh, in_specs=in_specs, out_specs=out_specs, check_vma=False)
```

time: 222 us -> 213 us (0.959)
  blocking collectives: 33.2 us -> 0 us
  starting transfers between devices: 45.3 us -> 75.9 us
  local copies, waits for them, and re-layouts: 33.9 us -> 16.6 us
  between operations: 0.28 us -> 13.6 us
  waiting for transfers between devices: 63.4 us -> 58.9 us
    all_to_all x8 -> x5, waiting for transfers between devices: 62 us -> 21.5 us  [the longest x2 21.5 us: body(): yx = lax.all_to_all(send, 'gx', 0, 0, tiled=True).reshape(256, RX * CH)]
    all_to_all x2 -> x0, blocking collectives: 33.2 us -> none  [the longest x1 24.8 us: gather_weights(): lax.all_to_all(own, 'gx', 0, 0, axis_index_groups=same_core, tiled=True)]
    ppermute x2 -> x15, starting transfers between devices: 0.6 us -> 29.3 us  [the longest x14 28.9 us: body(): zs.append(lax.ppermute(zy, 'gy', [(i, (i + s) % 8) for i in range(8)]))]
    all_gather x0 -> x2, waiting for transfers between devices: none -> 20.3 us  [the longest x1 20.3 us: body(): wx = lax.all_gather(own_x, 'gx', axis=0)]
    ppermute x2 -> x15, waiting for transfers between devices: 1.4 us -> 17 us  [the longest x14 17 us: body(): zs.append(lax.ppermute(zy, 'gy', [(i, (i + s) % 8) for i in range(8)]))]
    unnamed x59 -> x36, local copies, waits for them, and re-layouts: 20.6 us -> 14 us
    broadcast_in_dim x3 -> x1, local copies, waits for them, and re-layouts: 5.1 us -> 0.75 us  [body(): early = jnp.broadcast_to(own_x[0][None], (16, CH, 128))]
    reshape x1 -> x0, local copies, waits for them, and re-layouts: 2.94 us -> none  [body(): state = jnp.transpose(state_field[0], (2, 1, 0)).reshape(256, 4096)]
  transfers between devices with their start and end apart: 10 -> 22, of which waited for: 9 -> 7; matrix products, arithmetic and copies ran while one was open for 2% -> 1% of each run, Pallas kernels for 4% -> 15%
where the time goes in v2:
time: 213 us; the launch traced here: 211 us
  starting transfers between devices  75.9 us (36%)
  waiting for transfers between devices  58.9 us (28%)
  Pallas kernels  44.9 us (21%)
  local copies, waits for them, and re-layouts  16.6 us (8%)
  between operations  13.6 us (6%)
    ppermute x14, starting transfers between devices, body(): zs.append(lax.ppermute(zy, 'gy', [(i, (i + s) % 8) for i in range(8)]))  28.9 us
    pallas_call x2, Pallas kernels, last_call(): pl.pallas_call(functools.partial(last_kernel, more), name='last', grid=(8...  28.2 us
    all_to_all x2, waiting for transfers between devices, body(): yx = lax.all_to_all(send, 'gx', 0, 0, tiled=True).reshape(256, RX * CH)  21.5 us
    all_gather x1, waiting for transfers between devices, body(): wx = lax.all_gather(own_x, 'gx', axis=0)  20.3 us
    all_to_all x2, starting transfers between devices, body(): yx = lax.all_to_all(send, 'gx', 0, 0, tiled=True).reshape(256, RX * CH)  18.7 us
    ppermute x14, waiting for transfers between devices, body(): zs.append(lax.ppermute(zy, 'gy', [(i, (i + s) % 8) for i in range(8)]))  17 us
    all_to_all x2, starting transfers between devices, body(): recv = lax.all_to_all(zx.reshape(32, LINE, RX * CH), 'gx', 0, 0, tiled=True)  16 us
    unnamed x36, local copies, waits for them, and re-layouts  14 us
  transfers between devices with their start and end apart: 22, of which 7 were waited for; matrix products, arithmetic and copies ran while one was open for 1% of the time, Pallas kernels for 15%

profile of v2, /device:TPU:1, one launch (start us, length us, event | category | flops | bytes accessed | tf_op | source)
XLA Modules:
  0.0 211.5 jit_solution(349469815777236080)
XLA Ops:
  6.5 1.0 slice_bitcast_fusion.1
  7.5 0.8 pad_maximum_fusion
  8.3 0.0 all-gather.5.cloned.1.call-update
  8.3 0.8 slice_bitcast_fusion.2
  9.1 0.1 fusion.1
  9.2 0.8 broadcast_in_dim.11
  10.0 11.7 %all-to-all-start.1 = ((bf16[16,64,128]{2,1,0:T(8,128)(2,1)}), bf16[16,64,128]{2,1,0:T(8,128)(2,1)S(1)}, u32[]{:S(2)}, u32[]{:S(2)}) async-start(bf16[16,64,128]{2,1,0:T(8,128)(2,1)} %broadcast_in_dim.11), calls=%async_computation.1 | async-start | bytes 524288 | tf_op jit(solution)/shard_map/all_to_all | solution.py:409
  21.7 0.0 copy-start
  21.7 1.6 copy-done
  23.3 0.9 copy-done.9
  24.2 0.7 copy-done.10
  24.9 7.9 %first.1 = (bf16[640,4096]{1,0:T(8,128)(2,1)}, bf16[256,4096]{1,0:T(8,128)(2,1)S(1)}, bf16[256,640]{1,0:T(8,128)(2,1)}, bf16[24,4096]{1,0:T(8,128)(2,1)S(1)}) custom-call(bf16[64,64,256]{2,1,0:T(8,128)(2,1)S(1)} %bitcast.31, bf16[16,4096]{1,0:T(8,128)(2,1)S(1)} %copy-done.9, bf16[24,256]{1,0:T(8,128)(2,1)S(1)} %copy-done.10), custom_call_target="tpu_custom_call" | custom-call | flops 10000000000 | bytes 1048576 | tf_op jit(solution)/shard_map/first/pallas_call | solution.py:129
  32.8 1.3 copy-done.14
  34.1 0.0 all-to-all-done.1.w0_ref
  34.1 10.6 %all-to-all-start = ((bf16[32,8,640]{2,1,0:T(8,128)(2,1)}), bf16[32,8,640]{2,1,0:T(8,128)(2,1)S(1)}, u32[]{:S(2)}, u32[]{:S(2)}) async-start(bf16[32,8,640]{2,1,0:T(8,128)(2,1)} %bitcast.2), calls=%async_computation | async-start | bytes 655360 | tf_op jit(solution)/shard_map/all_to_all | solution.py:419
  44.8 0.3 collective-permute-start
  45.1 1.2 collective-permute-start.1
  46.3 2.4 %collective-permute-start.2 = (bf16[24,4096]{1,0:T(8,128)(2,1)S(1)}, bf16[24,4096]{1,0:T(8,128)(2,1)S(1)}, u32[]{:S(2)}, u32[]{:S(2)}) collective-permute-start(bf16[24,4096]{1,0:T(8,128)(2,1)S(1)} %get-tuple-element.14.refs_0_), channel_id=1, source_target_pairs={{0,2},{1,3},{2,4},{3,5},{4,6},{5,7},{6,0},{7,1},{8,10},{9,11},{10,... | collective-permute-start | bytes 589832 | tf_op jit(solution)/shard_map/ppermute | solution.py:418
  48.7 1.3 collective-permute-start.3
  50.0 1.1 collective-permute-start.4
  51.1 4.6 %collective-permute-done.1.refs_1_ = bf16[24,4096]{1,0:T(8,128)(2,1)S(1)} collective-permute-done((bf16[24,4096]{1,0:T(8,128)(2,1)S(1)}, bf16[24,4096]{1,0:T(8,128)(2,1)S(1)}, u32[]{:S(2)}, u32[]{:S(2)}) %collective-permute-start.1) | collective-permute-done | bytes 196640 | tf_op jit(solution)/shard_map/ppermute | solution.py:418
  55.7 0.0 collective-permute-start.5
  55.7 7.8 %collective-permute-done.2.refs_2_ = bf16[24,4096]{1,0:T(8,128)(2,1)S(1)} collective-permute-done((bf16[24,4096]{1,0:T(8,128)(2,1)S(1)}, bf16[24,4096]{1,0:T(8,128)(2,1)S(1)}, u32[]{:S(2)}, u32[]{:S(2)}) %collective-permute-start.2) | collective-permute-done | bytes 196640 | tf_op jit(solution)/shard_map/ppermute | solution.py:418
  63.4 0.0 collective-permute-start.6
  63.4 0.0 all-to-all-done.recv_ref
  63.5 0.0 copy-start.6
  63.5 2.2 %mid_x.2 = bf16[32,8,640]{2,1,0:T(8,128)(2,1)} custom-call(s32[1]{0:T(128)} %bitcast.core_ref.w1_ref, bf16[32,8,640]{2,1,0:T(8,128)(2,1)S(1)} %all-to-all-done.recv_ref, bf16[16,64,128]{2,1,0:T(8,128)(2,1)S(1)} %all-to-all-done.1.w0_ref, bf16[16,64,128]{2,1,0:T(8,128)(2,1)S(1)} %collective-permute-done.w1_ref, bf16[448,256]{1,0:T(8,128)(2,1)S(1)} %copy-done.7), custom_call_target="tpu_custom_call" | custom-call | flops 3000000000 | bytes 1048576 | tf_op jit(solution)/shard_map/mid_x/pallas_call | solution.py:219
  65.7 14.0 %all-to-all-start.2 = ((bf16[32,8,640]{2,1,0:T(8,128)(2,1)}), bf16[32,8,640]{2,1,0:T(8,128)(2,1)S(1)}, u32[]{:S(2)}, u32[]{:S(2)}) async-start(bf16[32,8,640]{2,1,0:T(8,128)(2,1)} %mid_x.2), calls=%async_computation.2 | async-start | bytes 655360 | tf_op jit(solution)/shard_map/all_to_all | solution.py:425
  79.7 0.2 all-gather.7.cloned.1.call-start
  80.0 0.7 pad_maximum_fusion.1
  80.7 0.0 all-gather.7.cloned.1.call-update
  80.7 0.0 collective-permute-done.4.refs_4_
  80.7 0.0 collective-permute-done.7.refs_7_
  80.7 0.0 all-gather.5.cloned.1.call-done
  80.8 1.2 copy-done.1
  82.0 2.2 %mid_y.2.refs_2_ = bf16[8,24,512]{2,1,0:T(8,128)(2,1)S(1)} custom-call(s32[1]{0:T(128)} %bitcast.7.me_ref, bf16[24,4096]{1,0:T(8,128)(2,1)S(1)} %get-tuple-element.14.refs_0_, bf16[24,4096]{1,0:T(8,128)(2,1)S(1)} %collective-permute-done.1.refs_1_, bf16[24,4096]{1,0:T(8,128)(2,1)S(1)} %collective-permute-done.2.refs_2_, ...), custom_call_target="tpu_custom_call" | custom-call | flops 6000000000 | bytes 1048576 | tf_op jit(solution)/shard_map/mid_y/pallas_call | solution.py:275
  84.2 10.0 %all-to-all-done.2 = bf16[32,8,640]{2,1,0:T(8,128)(2,1)S(1)} async-done(((bf16[32,8,640]{2,1,0:T(8,128)(2,1)}), bf16[32,8,640]{2,1,0:T(8,128)(2,1)S(1)}, u32[]{:S(2)}, u32[]{:S(2)}) %all-to-all-start.2) | async-done | bytes 327712 | tf_op jit(solution)/shard_map/all_to_all | solution.py:425
  94.2 0.0 copy-start.15
  94.2 1.6 copy-done.15
  95.8 15.7 %last.2 = (bf16[256,4096]{1,0:T(8,128)(2,1)S(1)}, bf16[256,640]{1,0:T(8,128)(2,1)}, bf16[24,4096]{1,0:T(8,128)(2,1)S(1)}) custom-call(bf16[256,640]{1,0:T(8,128)(2,1)S(1)} %bitcast.29, bf16[640,4096]{1,0:T(8,128)(2,1)} %get-tuple-element.13.refs_1_, bf16[8,24,512]{2,1,0:T(8,128)(2,1)S(1)} %mid_y.2.refs_2_, bf16[24,256]{1,0:T(8,128)(2,1)S(1)} %copy-done.11, ...), custom_call_target="tpu_custom_call" | custom-call | flops 12000000000 | bytes 1048576 | tf_op jit(solution)/shard_map/last/pallas_call | solution.py:385
  111.5 1.3 copy-done.12
  112.8 5.3 %all-to-all-start.3 = ((bf16[32,8,640]{2,1,0:T(8,128)(2,1)}), bf16[32,8,640]{2,1,0:T(8,128)(2,1)S(1)}, u32[]{:S(2)}, u32[]{:S(2)}) async-start(bf16[32,8,640]{2,1,0:T(8,128)(2,1)} %bitcast.12), calls=%async_computation.3 | async-start | bytes 655360 | tf_op jit(solution)/shard_map/all_to_all | solution.py:419
  118.2 0.1 collective-permute-start.10
  118.2 0.2 collective-permute-start.11
  118.4 2.3 %collective-permute-start.12 = (bf16[24,4096]{1,0:T(8,128)(2,1)S(1)}, bf16[24,4096]{1,0:T(8,128)(2,1)S(1)}, u32[]{:S(2)}, u32[]{:S(2)}) collective-permute-start(bf16[24,4096]{1,0:T(8,128)(2,1)S(1)} %get-tuple-element.17.refs_0_), channel_id=1, source_target_pairs={{0,5},{1,6},{2,7},{3,0},{4,1},{5,2},{6,3},{7,4},{8,13},{9,14},{10,... | collective-permute-start | bytes 589832 | tf_op jit(solution)/shard_map/ppermute | solution.py:418
  120.7 3.7 %collective-permute-start.13 = (bf16[24,4096]{1,0:T(8,128)(2,1)S(1)}, bf16[24,4096]{1,0:T(8,128)(2,1)S(1)}, u32[]{:S(2)}, u32[]{:S(2)}) collective-permute-start(bf16[24,4096]{1,0:T(8,128)(2,1)S(1)} %get-tuple-element.17.refs_0_), channel_id=1, source_target_pairs={{0,6},{1,7},{2,0},{3,1},{4,2},{5,3},{6,4},{7,5},{8,14},{9,15},{10,... | collective-permute-start | bytes 589832 | tf_op jit(solution)/shard_map/ppermute | solution.py:418
  124.3 0.3 collective-permute-start.14
  124.7 2.1 %collective-permute-done.10.refs_3_ = bf16[24,4096]{1,0:T(8,128)(2,1)S(1)} collective-permute-done((bf16[24,4096]{1,0:T(8,128)(2,1)S(1)}, bf16[24,4096]{1,0:T(8,128)(2,1)S(1)}, u32[]{:S(2)}, u32[]{:S(2)}) %collective-permute-start.10) | collective-permute-done | bytes 196640 | tf_op jit(solution)/shard_map/ppermute | solution.py:418
  126.8 2.9 %collective-permute-start.8 = (bf16[24,4096]{1,0:T(8,128)(2,1)S(1)}, bf16[24,4096]{1,0:T(8,128)(2,1)S(1)}, u32[]{:S(2)}, u32[]{:S(2)}) collective-permute-start(bf16[24,4096]{1,0:T(8,128)(2,1)S(1)} %get-tuple-element.17.refs_0_), channel_id=1, source_target_pairs={{0,1},{1,2},{2,3},{3,4},{4,5},{5,6},{6,7},{7,0},{8,9},{9,10},{10,1... | collective-permute-start | bytes 589832 | tf_op jit(solution)/shard_map/ppermute | solution.py:418
  129.7 2.5 %collective-permute-done.11.refs_4_ = bf16[24,4096]{1,0:T(8,128)(2,1)S(1)} collective-permute-done((bf16[24,4096]{1,0:T(8,128)(2,1)S(1)}, bf16[24,4096]{1,0:T(8,128)(2,1)S(1)}, u32[]{:S(2)}, u32[]{:S(2)}) %collective-permute-start.11) | collective-permute-done | bytes 196640 | tf_op jit(solution)/shard_map/ppermute | solution.py:418
  132.3 13.5 %collective-permute-start.9 = (bf16[24,4096]{1,0:T(8,128)(2,1)S(1)}, bf16[24,4096]{1,0:T(8,128)(2,1)S(1)}, u32[]{:S(2)}, u32[]{:S(2)}) collective-permute-start(bf16[24,4096]{1,0:T(8,128)(2,1)S(1)} %get-tuple-element.17.refs_0_), channel_id=1, source_target_pairs={{0,2},{1,3},{2,4},{3,5},{4,6},{5,7},{6,0},{7,1},{8,10},{9,11},{10,... | collective-permute-start | bytes 589832 | tf_op jit(solution)/shard_map/ppermute | solution.py:418
  145.8 20.3 %all-gather.7.cloned.1.call-done = bf16[64,1,64,128]{3,2,1,0:T(8,128)(2,1)} async-done(((bf16[2,1,64,128]{3,2,1,0:T(8,128)(2,1)}), bf16[64,1,64,128]{3,2,1,0:T(8,128)(2,1)}) %all-gather.7.cloned.1.call-update) | async-done | bytes 1048592 | tf_op jit(solution)/shard_map/all_gather | solution.py:412
  166.1 1.2 copy-done.3
  167.3 0.9 copy-done.8
  168.2 2.2 %mid_x.3 = bf16[32,8,640]{2,1,0:T(8,128)(2,1)} custom-call(s32[1]{0:T(128)} %bitcast.core_ref.w1_ref, bf16[32,8,640]{2,1,0:T(8,128)(2,1)S(1)} %all-to-all-done.3.recv_ref, bf16[32,2,64,128]{3,2,1,0:T(8,128)(2,1)S(1)} %bitcast.34, s32[1]{0:T(128)} %bitcast.core_ref.w1_ref, bf16[448,256]{1,0:T(8,128)(2,1)S(1)} %copy-done.8), custom_call_target="tpu_custom_call" | custom-call | flops 3000000000 | bytes 1048576 | tf_op jit(solution)/shard_map/mid_x/pallas_call | solution.py:219
  170.4 4.7 %all-to-all-start.4 = ((bf16[32,8,640]{2,1,0:T(8,128)(2,1)}), bf16[32,8,640]{2,1,0:T(8,128)(2,1)S(1)}, u32[]{:S(2)}, u32[]{:S(2)}) async-start(bf16[32,8,640]{2,1,0:T(8,128)(2,1)} %mid_x.3), calls=%async_computation.4 | async-start | bytes 655360 | tf_op jit(solution)/shard_map/all_to_all | solution.py:425
  175.1 0.0 collective-permute-done.12.refs_5_
  175.1 0.0 collective-permute-done.14.refs_7_
  175.2 2.2 %mid_y.3.refs_2_ = bf16[8,24,512]{2,1,0:T(8,128)(2,1)S(1)} custom-call(s32[1]{0:T(128)} %bitcast.7.me_ref, bf16[24,4096]{1,0:T(8,128)(2,1)S(1)} %get-tuple-element.17.refs_0_, bf16[24,4096]{1,0:T(8,128)(2,1)S(1)} %collective-permute-done.8.refs_1_, bf16[24,4096]{1,0:T(8,128)(2,1)S(1)} %collective-permute-done.9.refs_2_, ...), custom_call_target="tpu_custom_call" | custom-call | flops 6000000000 | bytes 1048576 | tf_op jit(solution)/shard_map/mid_y/pallas_call | solution.py:275
  177.4 0.7 copy-done.16
  178.1 11.5 %all-to-all-done.4 = bf16[32,8,640]{2,1,0:T(8,128)(2,1)S(1)} async-done(((bf16[32,8,640]{2,1,0:T(8,128)(2,1)}), bf16[32,8,640]{2,1,0:T(8,128)(2,1)S(1)}, u32[]{:S(2)}, u32[]{:S(2)}) %all-to-all-start.4) | async-done | bytes 327712 | tf_op jit(solution)/shard_map/all_to_all | solution.py:425
  189.6 1.6 copy-done.13
  191.2 0.9 copy-done.17
  192.1 12.6 %last.3 = bf16[64,64,256]{2,1,0:T(8,128)(2,1)} custom-call(bf16[256,640]{1,0:T(8,128)(2,1)S(1)} %bitcast.30, bf16[640,4096]{1,0:T(8,128)(2,1)} %get-tuple-element.13.refs_1_, bf16[8,24,512]{2,1,0:T(8,128)(2,1)S(1)} %copy-done.17, bf16[24,256]{1,0:T(8,128)(2,1)S(1)} %copy-done.11, bf16[256,4096]{1,0:T(8,128)(2,1)S(1)} %copy-done.13, ...), custom_call_target="tpu_custom_call" | custom-call | flops 12000000000 | bytes 1048576 | tf_op jit(solution)/shard_map/last/pallas_call | solution.py:385
  (31 shorter events, 0.1 us)
Async XLA Ops:
  6.5 74.2 %all-gather.5.cloned.1.call-start = ((), (), s32[]{:S(2)}) async-start(), calls=%async_computation.5 | async-start | bytes 1179648 | tf_op jit(solution)/shard_map/all_gather | solution.py:411
  10.0 24.2 %all-to-all-start.1 = ((bf16[16,64,128]{2,1,0:T(8,128)(2,1)}), bf16[16,64,128]{2,1,0:T(8,128)(2,1)S(1)}, u32[]{:S(2)}, u32[]{:S(2)}) async-start(bf16[16,64,128]{2,1,0:T(8,128)(2,1)} %broadcast_in_dim.11), calls=%async_computation.1 | async-start | bytes 524288 | tf_op jit(solution)/shard_map/all_to_all | solution.py:409
  21.7 1.6 copy-start
  23.3 0.9 copy-start.9
  24.2 0.7 copy-start.10
  24.9 38.5 %copy-start.7 = (bf16[448,256]{1,0:T(8,128)(2,1)S(1)}, bf16[448,256]{1,0:T(8,128)(2,1)}, u32[]{:S(2)}) copy-start(bf16[448,256]{1,0:T(8,128)(2,1)} %constant.22.clone.tab_ref) | copy-start | bytes 688132
  32.8 1.3 copy-start.14
  34.1 29.3 %all-to-all-start = ((bf16[32,8,640]{2,1,0:T(8,128)(2,1)}), bf16[32,8,640]{2,1,0:T(8,128)(2,1)S(1)}, u32[]{:S(2)}, u32[]{:S(2)}) async-start(bf16[32,8,640]{2,1,0:T(8,128)(2,1)} %bitcast.2), calls=%async_computation | async-start | bytes 655360 | tf_op jit(solution)/shard_map/all_to_all | solution.py:419
  44.8 18.7 %collective-permute-start = (bf16[16,64,128]{2,1,0:T(8,128)(2,1)S(1)}, bf16[16,64,128]{2,1,0:T(8,128)(2,1)S(1)}, u32[]{:S(2)}, u32[]{:S(2)}) collective-permute-start(bf16[16,64,128]{2,1,0:T(8,128)(2,1)S(1)} %all-to-all-done.1.w0_ref), channel_id=1, source_target_pairs={{0,8},{8,0},{16,24},{24,16},{32,40},{40,32},{48,56},{56,48},{64,72... | collective-permute-start | bytes 786440 | tf_op jit(solution)/shard_map/ppermute | solution.py:410
  45.1 10.6 %collective-permute-start.1 = (bf16[24,4096]{1,0:T(8,128)(2,1)S(1)}, bf16[24,4096]{1,0:T(8,128)(2,1)S(1)}, u32[]{:S(2)}, u32[]{:S(2)}) collective-permute-start(bf16[24,4096]{1,0:T(8,128)(2,1)S(1)} %get-tuple-element.14.refs_0_), channel_id=1, source_target_pairs={{0,1},{1,2},{2,3},{3,4},{4,5},{5,6},{6,7},{7,0},{8,9},{9,10},{10,1... | collective-permute-start | bytes 589832 | tf_op jit(solution)/shard_map/ppermute | solution.py:418
  46.3 17.1 %collective-permute-start.2 = (bf16[24,4096]{1,0:T(8,128)(2,1)S(1)}, bf16[24,4096]{1,0:T(8,128)(2,1)S(1)}, u32[]{:S(2)}, u32[]{:S(2)}) collective-permute-start(bf16[24,4096]{1,0:T(8,128)(2,1)S(1)} %get-tuple-element.14.refs_0_), channel_id=1, source_target_pairs={{0,2},{1,3},{2,4},{3,5},{4,6},{5,7},{6,0},{7,1},{8,10},{9,11},{10,... | collective-permute-start | bytes 589832 | tf_op jit(solution)/shard_map/ppermute | solution.py:418
  48.7 32.0 %collective-permute-start.3 = (bf16[24,4096]{1,0:T(8,128)(2,1)S(1)}, bf16[24,4096]{1,0:T(8,128)(2,1)S(1)}, u32[]{:S(2)}, u32[]{:S(2)}) collective-permute-start(bf16[24,4096]{1,0:T(8,128)(2,1)S(1)} %get-tuple-element.14.refs_0_), channel_id=1, source_target_pairs={{0,3},{1,4},{2,5},{3,6},{4,7},{5,0},{6,1},{7,2},{8,11},{9,12},{10,... | collective-permute-start | bytes 589832 | tf_op jit(solution)/shard_map/ppermute | solution.py:418
  50.0 30.7 %collective-permute-start.4 = (bf16[24,4096]{1,0:T(8,128)(2,1)S(1)}, bf16[24,4096]{1,0:T(8,128)(2,1)S(1)}, u32[]{:S(2)}, u32[]{:S(2)}) collective-permute-start(bf16[24,4096]{1,0:T(8,128)(2,1)S(1)} %get-tuple-element.14.refs_0_), channel_id=1, source_target_pairs={{0,4},{1,5},{2,6},{3,7},{4,0},{5,1},{6,2},{7,3},{8,12},{9,13},{10,... | collective-permute-start | bytes 589832 | tf_op jit(solution)/shard_map/ppermute | solution.py:418
  55.7 25.1 %collective-permute-start.5 = (bf16[24,4096]{1,0:T(8,128)(2,1)S(1)}, bf16[24,4096]{1,0:T(8,128)(2,1)S(1)}, u32[]{:S(2)}, u32[]{:S(2)}) collective-permute-start(bf16[24,4096]{1,0:T(8,128)(2,1)S(1)} %get-tuple-element.14.refs_0_), channel_id=1, source_target_pairs={{0,5},{1,6},{2,7},{3,0},{4,1},{5,2},{6,3},{7,4},{8,13},{9,14},{10,... | collective-permute-start | bytes 589832 | tf_op jit(solution)/shard_map/ppermute | solution.py:418
  63.4 17.3 %collective-permute-start.6 = (bf16[24,4096]{1,0:T(8,128)(2,1)S(1)}, bf16[24,4096]{1,0:T(8,128)(2,1)S(1)}, u32[]{:S(2)}, u32[]{:S(2)}) collective-permute-start(bf16[24,4096]{1,0:T(8,128)(2,1)S(1)} %get-tuple-element.14.refs_0_), channel_id=1, source_target_pairs={{0,6},{1,7},{2,0},{3,1},{4,2},{5,3},{6,4},{7,5},{8,14},{9,15},{10,... | collective-permute-start | bytes 589832 | tf_op jit(solution)/shard_map/ppermute | solution.py:418
  63.4 17.3 %collective-permute-start.7 = (bf16[24,4096]{1,0:T(8,128)(2,1)S(1)}, bf16[24,4096]{1,0:T(8,128)(2,1)S(1)}, u32[]{:S(2)}, u32[]{:S(2)}) collective-permute-start(bf16[24,4096]{1,0:T(8,128)(2,1)S(1)} %get-tuple-element.14.refs_0_), channel_id=1, source_target_pairs={{0,7},{1,0},{2,1},{3,2},{4,3},{5,4},{6,5},{7,6},{8,15},{9,8},{10,9... | collective-permute-start | bytes 589832 | tf_op jit(solution)/shard_map/ppermute | solution.py:418
  63.5 17.3 %copy-start.6 = (bf16[8,96,256]{2,1,0:T(8,128)(2,1)S(1)}, bf16[8,96,256]{2,1,0:T(8,128)(2,1)}, u32[]{:S(2)}) copy-start(bf16[8,96,256]{2,1,0:T(8,128)(2,1)} %constant.23.clone.refs_9_) | copy-start | bytes 1179652
  65.7 28.5 %all-to-all-start.2 = ((bf16[32,8,640]{2,1,0:T(8,128)(2,1)}), bf16[32,8,640]{2,1,0:T(8,128)(2,1)S(1)}, u32[]{:S(2)}, u32[]{:S(2)}) async-start(bf16[32,8,640]{2,1,0:T(8,128)(2,1)} %mid_x.2), calls=%async_computation.2 | async-start | bytes 655360 | tf_op jit(solution)/shard_map/all_to_all | solution.py:425
  79.7 86.3 %all-gather.7.cloned.1.call-start = ((), (), s32[]{:S(2)}) async-start(), calls=%async_computation.6 | async-start | bytes 1081344 | tf_op jit(solution)/shard_map/all_gather | solution.py:412
  80.8 1.2 copy-start.1
  82.0 12.2 %copy-start.4 = (bf16[2,64,256]{2,1,0:T(8,128)(2,1)S(1)}, bf16[2,64,256]{2,1,0:T(8,128)(2,1)}, u32[]{:S(2)}) copy-start(bf16[2,64,256]{2,1,0:T(8,128)(2,1)} %refs_5_.3) | copy-start | bytes 196612
  82.0 12.2 %copy-start.5 = (bf16[2,256,64]{1,2,0:T(8,128)(2,1)S(1)}, bf16[2,256,64]{1,2,0:T(8,128)(2,1)}, u32[]{:S(2)}) copy-start(bf16[2,256,64]{1,2,0:T(8,128)(2,1)} %param.13) | copy-start | bytes 196612
  82.0 12.2 %copy-start.11 = (bf16[24,256]{1,0:T(8,128)(2,1)S(1)}, bf16[24,256]{1,0:T(8,128)(2,1)}, u32[]{:S(2)}) copy-start(bf16[24,256]{1,0:T(8,128)(2,1)} %constant.24.clone.cy_ref.refs_3_) | copy-start | bytes 36868
  94.2 1.6 copy-start.15
  111.5 1.3 copy-start.12
  112.8 53.3 %all-to-all-start.3 = ((bf16[32,8,640]{2,1,0:T(8,128)(2,1)}), bf16[32,8,640]{2,1,0:T(8,128)(2,1)S(1)}, u32[]{:S(2)}, u32[]{:S(2)}) async-start(bf16[32,8,640]{2,1,0:T(8,128)(2,1)} %bitcast.12), calls=%async_computation.3 | async-start | bytes 655360 | tf_op jit(solution)/shard_map/all_to_all | solution.py:419
  118.2 8.7 %collective-permute-start.10 = (bf16[24,4096]{1,0:T(8,128)(2,1)S(1)}, bf16[24,4096]{1,0:T(8,128)(2,1)S(1)}, u32[]{:S(2)}, u32[]{:S(2)}) collective-permute-start(bf16[24,4096]{1,0:T(8,128)(2,1)S(1)} %get-tuple-element.17.refs_0_), channel_id=1, source_target_pairs={{0,3},{1,4},{2,5},{3,6},{4,7},{5,0},{6,1},{7,2},{8,11},{9,12},{10,... | collective-permute-start | bytes 589832 | tf_op jit(solution)/shard_map/ppermute | solution.py:418
  118.2 14.0 %collective-permute-start.11 = (bf16[24,4096]{1,0:T(8,128)(2,1)S(1)}, bf16[24,4096]{1,0:T(8,128)(2,1)S(1)}, u32[]{:S(2)}, u32[]{:S(2)}) collective-permute-start(bf16[24,4096]{1,0:T(8,128)(2,1)S(1)} %get-tuple-element.17.refs_0_), channel_id=1, source_target_pairs={{0,4},{1,5},{2,6},{3,7},{4,0},{5,1},{6,2},{7,3},{8,12},{9,13},{10,... | collective-permute-start | bytes 589832 | tf_op jit(solution)/shard_map/ppermute | solution.py:418
  118.4 56.7 %collective-permute-start.12 = (bf16[24,4096]{1,0:T(8,128)(2,1)S(1)}, bf16[24,4096]{1,0:T(8,128)(2,1)S(1)}, u32[]{:S(2)}, u32[]{:S(2)}) collective-permute-start(bf16[24,4096]{1,0:T(8,128)(2,1)S(1)} %get-tuple-element.17.refs_0_), channel_id=1, source_target_pairs={{0,5},{1,6},{2,7},{3,0},{4,1},{5,2},{6,3},{7,4},{8,13},{9,14},{10,... | collective-permute-start | bytes 589832 | tf_op jit(solution)/shard_map/ppermute | solution.py:418
  120.7 54.4 %collective-permute-start.13 = (bf16[24,4096]{1,0:T(8,128)(2,1)S(1)}, bf16[24,4096]{1,0:T(8,128)(2,1)S(1)}, u32[]{:S(2)}, u32[]{:S(2)}) collective-permute-start(bf16[24,4096]{1,0:T(8,128)(2,1)S(1)} %get-tuple-element.17.refs_0_), channel_id=1, source_target_pairs={{0,6},{1,7},{2,0},{3,1},{4,2},{5,3},{6,4},{7,5},{8,14},{9,15},{10,... | collective-permute-start | bytes 589832 | tf_op jit(solution)/shard_map/ppermute | solution.py:418
  124.3 50.8 %collective-permute-start.14 = (bf16[24,4096]{1,0:T(8,128)(2,1)S(1)}, bf16[24,4096]{1,0:T(8,128)(2,1)S(1)}, u32[]{:S(2)}, u32[]{:S(2)}) collective-permute-start(bf16[24,4096]{1,0:T(8,128)(2,1)S(1)} %get-tuple-element.17.refs_0_), channel_id=1, source_target_pairs={{0,7},{1,0},{2,1},{3,2},{4,3},{5,4},{6,5},{7,6},{8,15},{9,8},{10,9... | collective-permute-start | bytes 589832 | tf_op jit(solution)/shard_map/ppermute | solution.py:418
  126.8 48.3 %collective-permute-start.8 = (bf16[24,4096]{1,0:T(8,128)(2,1)S(1)}, bf16[24,4096]{1,0:T(8,128)(2,1)S(1)}, u32[]{:S(2)}, u32[]{:S(2)}) collective-permute-start(bf16[24,4096]{1,0:T(8,128)(2,1)S(1)} %get-tuple-element.17.refs_0_), channel_id=1, source_target_pairs={{0,1},{1,2},{2,3},{3,4},{4,5},{5,6},{6,7},{7,0},{8,9},{9,10},{10,1... | collective-permute-start | bytes 589832 | tf_op jit(solution)/shard_map/ppermute | solution.py:418
  132.3 42.9 %collective-permute-start.9 = (bf16[24,4096]{1,0:T(8,128)(2,1)S(1)}, bf16[24,4096]{1,0:T(8,128)(2,1)S(1)}, u32[]{:S(2)}, u32[]{:S(2)}) collective-permute-start(bf16[24,4096]{1,0:T(8,128)(2,1)S(1)} %get-tuple-element.17.refs_0_), channel_id=1, source_target_pairs={{0,2},{1,3},{2,4},{3,5},{4,6},{5,7},{6,0},{7,1},{8,10},{9,11},{10,... | collective-permute-start | bytes 589832 | tf_op jit(solution)/shard_map/ppermute | solution.py:418
  166.1 1.2 copy-start.3
  167.3 0.9 copy-start.8
  168.2 6.9 %copy-start.2 = (bf16[16,4,64,128]{3,2,1,0:T(8,128)(2,1)S(1)}, bf16[16,4,64,128]{3,2,1,0:T(8,128)(2,1)}, u32[]{:S(2)}) copy-start(bf16[16,4,64,128]{3,2,1,0:T(8,128)(2,1)} %all-gather.5.cloned.1.call-done) | copy-start | bytes 3145732
  170.4 19.1 %all-to-all-start.4 = ((bf16[32,8,640]{2,1,0:T(8,128)(2,1)}), bf16[32,8,640]{2,1,0:T(8,128)(2,1)S(1)}, u32[]{:S(2)}, u32[]{:S(2)}) async-start(bf16[32,8,640]{2,1,0:T(8,128)(2,1)} %mid_x.3), calls=%async_computation.4 | async-start | bytes 655360 | tf_op jit(solution)/shard_map/all_to_all | solution.py:425
  177.4 0.7 copy-start.16
  189.6 1.6 copy-start.13
  191.2 0.9 copy-start.17
Sparse Core Ops, SparseCore 0:
  9.1 40.5 all-gather.4
  83.4 82.6 all-gather.6
